TPU v7x, 512 devices: a whole 4x8x8 slice. The times are simulated.
512 devices in a mesh: member: 4 (over x), gx: 16 (over z, core), gy: 8 (over y).
Axes of the slice: x: 4, y: 8, z: 8, core: 2. Of those that a mesh axis runs over, the one named last changes fastest.
Arguments:
- background: float32 [4, 16, 1024, 1024], P('member', None, 'gx', 'gy'), may hold values from -6 to 6
- mixing: float32 [4, 4], replicated, may hold values from 0.1 to 0.6
- kappa_sq: float32 [16, 1024, 1024], P(None, 'gx', 'gy'), may hold values from 0.05 to 1
- scaling: float32 [16, 1024, 1024], P(None, 'gx', 'gy'), may hold values from 0.5 to 2
- line_inverse: float32 [16, 4, 256, 256], P('gx'), may hold values from -3 to 3
- panels: float32 [16, 65536], P(None, ('gx', 'gy')), may hold values from -3 to 3
- values: float32 [4, 65536], P('member', ('gx', 'gy')), may hold values from -6 to 6
- targets: int32 [65536, 1], P(('gx', 'gy')), may hold values from 0 to 127; in each aligned block of 512 rows (0 to 511, 512 to 1023, ...) at most 8 rows name the same one
- spots: int32 [65536], P(('gx', 'gy')), may hold values from 0 to 8191
Outputs:
- posterior: float32 [4, 16, 1024, 1024], P('member', None, 'gx', 'gy')
Inputs may be any that keep to these rules, and one draw needn't show every extreme that they name: `targets`: among the 512 stations of one device (aligned blocks) no tile is named more than 8 times. `spots`: a column x * 128 + y of the tile's plane.
All inputs are finite; a program needn't handle non-finite values.
Results may differ from a plain program's by a relative error of at most 0.00011.
Values sent between devices are 32-bit elements; how exact they have to be, the bound alone decides.
A program may use at most 64 MiB of HBM per device.

v0:
```python
import jax
import jax.numpy as jnp
from jax import lax
from jax.sharding import PartitionSpec as P


def with_halo(block, sides, width):
    for axis, dim in sides:
        count = lax.axis_size(axis)
        forward = [(i, i + 1) for i in range(count - 1)]
        backward = [(target, source) for source, target in forward]
        low = lax.ppermute(
            lax.slice_in_dim(block, block.shape[dim] - width, None, axis=dim), axis, forward
        )
        high = lax.ppermute(lax.slice_in_dim(block, 0, width, axis=dim), axis, backward)
        block = jnp.concatenate([low, block, high], axis=dim)
    return block


def shards(background, mixing, kappa_sq, scaling, line_inverse, panels, values, targets, spots):
    highest = lax.Precision.HIGHEST
    depth, width_x, width_y = kappa_sq.shape
    member = lax.axis_index("member")
    column_weights = lax.dynamic_slice_in_dim(mixing, member, 1, 1)[:, 0]
    picked = column_weights
    prior = lax.psum_scatter(
        picked[:, None, None, None] * background, "member", scatter_dimension=0, tiled=True
    )
    grid_x = lax.axis_size("gx")
    grid_y = lax.axis_size("gy")
    tile_count = grid_x * grid_y
    station_count = spots.shape[0]
    slot_cap = max(2, 2 * station_count // tile_count)
    owner = targets[:, 0]
    hits = (owner[:, None] == jnp.arange(tile_count, dtype=jnp.int32)[None, :]).astype(jnp.float32)
    order = jnp.arange(station_count, dtype=jnp.int32)
    earlier = (order[:, None] > order[None, :]).astype(jnp.float32)
    before = jnp.dot(earlier, hits, preferred_element_type=jnp.float32)
    rank = jnp.sum(before * hits, axis=1).astype(jnp.int32)
    slot_index = owner * slot_cap + rank
    slot_ids = jnp.arange(tile_count * slot_cap, dtype=jnp.int32)
    placing = (slot_ids[:, None] == slot_index[None, :]).astype(jnp.float32)
    sent_panels = jnp.dot(placing, panels.T, precision=highest)
    extras = jnp.stack([values[0], spots.astype(jnp.float32)], axis=1)
    sent_extra = jnp.dot(placing, extras, precision=highest)
    got_panels, got_extra = (
        lax.all_to_all(
            sent_panels.reshape(tile_count, slot_cap * depth),
            ("gx", "gy"),
            split_axis=0,
            concat_axis=0,
            tiled=True,
        ),
        lax.all_to_all(
            sent_extra.reshape(tile_count, slot_cap * 2),
            ("gx", "gy"),
            split_axis=0,
            concat_axis=0,
            tiled=True,
        ),
    )
    recv_panels = got_panels.reshape(-1, depth).T
    recv_extra = got_extra.reshape(-1, 2)
    observations = recv_extra[:, 0]
    cells = recv_extra[:, 1].astype(jnp.int32)

    def station_sum(weights):
        flat = jnp.zeros((depth, width_x * width_y), jnp.float32)
        flat = flat.at[:, cells].add(recv_panels * weights[None, :])
        return flat.reshape(1, depth, width_x, width_y)

    def observed(field):
        picked = field.reshape(depth, width_x * width_y)[:, cells]
        return station_sum(jnp.sum(recv_panels * picked, axis=0))

    line = line_inverse.shape[2]

    def solve_lines(pencil):
        levels, full_x, across = (pencil.shape[1], pencil.shape[2], pencil.shape[3])
        blocks = pencil.reshape(1, levels, full_x // line, line, across)
        solved = jnp.einsum("zbij,mzbjy->mzbiy", line_inverse, blocks, precision=highest)
        solved = solved.reshape(1, levels, full_x, across)
        return lax.all_to_all(solved, "gx", split_axis=2, concat_axis=1, tiled=True)

    def precondition(resid):
        return solve_lines(lax.all_to_all(resid, "gx", split_axis=1, concat_axis=2, tiled=True))

    forcing = station_sum(observations)
    first = precondition(forcing - observed(prior))
    scaled = scaling[None] * first
    rimmed = with_halo(scaled, (("gx", 2), ("gy", 3)), 1)
    padded = jnp.pad(rimmed, ((0, 0), (1, 1), (0, 0), (0, 0)))
    beside = padded[:, 2:, 1:-1, 1:-1] + padded[:, :-2, 1:-1, 1:-1]
    beside = beside + padded[:, 1:-1, 2:, 1:-1] + padded[:, 1:-1, :-2, 1:-1]
    beside = beside + padded[:, 1:-1, 1:-1, 2:] + padded[:, 1:-1, 1:-1, :-2]
    second = first + precondition(
        forcing
        - observed(prior + first)
        - (kappa_sq[None] * first + scaling[None] * (6.0 * scaled - beside))
    )
    return prior + second


def solution(mesh):
    return jax.shard_map(
        shards,
        mesh=mesh,
        in_specs=(
            P("member", None, "gx", "gy"),
            P(),
            P(None, "gx", "gy"),
            P(None, "gx", "gy"),
            P("gx", None, None, None),
            P(None, ("gx", "gy")),
            P("member", ("gx", "gy")),
            P(("gx", "gy"), None),
            P(("gx", "gy")),
        ),
        out_specs=P("member", None, "gx", "gy"),
        check_vma=False,
    )
```

profile of v0, /device:TPU:1, one launch (start us, length us, event | category | flops | bytes accessed | tf_op | source)
XLA Modules:
  0.0 236.1 jit_solution(16545074111539085819)
XLA Ops:
  7.5 2.7 %broadcast_multiply_fusion = f32[4,16,64,128]{3,2,1,0:T(8,128)} fusion(f32[16,64,128]{2,1,0:T(8,128)} %bitcast.58, f32[4]{0:T(128)S(1)} %dynamic-slice_reduce_fusion), kind=kLoop, calls=%fused_computation.31 | loop fusion | flops 524288 | bytes 2621456 | tf_op jit(solution)/shard_map/mul | solution.py:27
  12.4 18.4 %all-to-all-start = ((f32[128,1,16]{2,1,0:T(1,128)}), f32[128,1,16]{2,1,0:T(1,128)S(1)}, u32[]{:S(2)}, u32[]{:S(2)}) async-start(f32[128,1,16]{2,1,0:T(1,128)} %bitcast.4), calls=%async_computation.1 | async-start | bytes 131072 | tf_op jit(solution)/shard_map/all_to_all | solution.py:54
  32.7 9.4 %all-to-all-done = f32[128,1,16]{2,1,0:T(1,128)S(1)} async-done(((f32[128,1,16]{2,1,0:T(1,128)}), f32[128,1,16]{2,1,0:T(1,128)S(1)}, u32[]{:S(2)}, u32[]{:S(2)}) %all-to-all-start) | async-done | bytes 8224 | tf_op jit(solution)/shard_map/all_to_all | solution.py:54
  42.1 6.3 %all-to-all-start.1 = ((f32[128,1,128]{2,1,0:T(1,128)}), f32[128,1,128]{2,1,0:T(1,128)S(1)}, u32[]{:S(2)}, u32[]{:S(2)}) async-start(f32[128,1,128]{2,1,0:T(1,128)} %bitcast.5), calls=%async_computation.2 | async-start | bytes 131072 | tf_op jit(solution)/shard_map/all_to_all | solution.py:47
  50.5 9.3 %all-to-all-done.1 = f32[128,1,128]{2,1,0:T(1,128)S(1)} async-done(((f32[128,1,128]{2,1,0:T(1,128)}), f32[128,1,128]{2,1,0:T(1,128)S(1)}, u32[]{:S(2)}, u32[]{:S(2)}) %all-to-all-start.1) | async-done | bytes 65568 | tf_op jit(solution)/shard_map/all_to_all | solution.py:47
  60.7 8.7 %scatter_custom_fusion = f32[16,8192]{0,1:T(8,128)} fusion(s32[1024]{0:T(1024)S(1)} %fusion.14, f32[]{:T(128)} %constant.6.clone.1, f32[1024,16]{1,0:T(8,128)S(1)} %reshape.142, f32[1024]{0:T(1024)S(1)} %slice_reduce_fusion), kind=kCustom, calls=%fused_computation.14 | custom fusion | flops 32768 | bytes 1052676 | tf_op jit(solution)/shard_map/scatter-add | solution.py:69
  69.4 3.5 %copy.47 = f32[1,16,64,128]{1,3,2,0:T(8,128)} copy(f32[1,16,64,128]{3,2,1,0:T(8,128)} %reduce-scatter.2.cloned.1.call-done) | data formatting | bytes 1048576 | tf_op jit(solution)/shard_map/reduce_scatter | solution.py:26
  73.0 5.0 %gather_fusion = f32[1024,16]{1,0:T(8,128)S(1)} fusion(f32[16,8192]{0,1:T(8,128)} %bitcast.52, s32[1024]{0:T(1024)S(1)} %broadcast_clamp_fusion), kind=kCustom, calls=%fused_computation | custom fusion | bytes 135168 | tf_op jit(solution)/shard_map/gather | solution.py:73
  78.2 8.7 %scatter_custom_fusion.1 = f32[16,8192]{0,1:T(8,128)} fusion(s32[1024]{0:T(1024)S(1)} %fusion.14, f32[]{:T(128)} %constant.6.clone.1, f32[1024,16]{1,0:T(8,128)S(1)} %reshape.142, f32[1024]{0:T(1024)S(1)} %multiply_reduce_fusion.1), kind=kCustom, calls=%fused_computation.12 | custom fusion | flops 32768 | bytes 1052676 | tf_op jit(solution)/shard_map/scatter-add | solution.py:69
  86.9 5.9 %sub.34 = f32[16,8192]{0,1:T(8,128)} subtract(f32[16,8192]{0,1:T(8,128)} %scatter_custom_fusion, f32[16,8192]{0,1:T(8,128)} %scatter_custom_fusion.1) | non-fusion elementwise | flops 131072 | bytes 1572864 | tf_op jit(solution)/shard_map/sub | solution.py:89
  92.8 2.9 %copy.48 = f32[1,16,64,128]{3,2,0,1:T(8,128)S(1)} copy(f32[1,16,64,128]{1,3,2,0:T(8,128)} %bitcast.46) | data formatting | bytes 1048576 | tf_op jit(solution)/shard_map/sub | solution.py:89
  95.7 20.9 %all_to_all.63 = f32[1,16,64,128]{3,2,0,1:T(8,128)S(1)} all-to-all(f32[1,16,64,128]{3,2,0,1:T(8,128)S(1)} %copy.48), channel_id=1, replica_groups=mesh['member'=4,'gx'=16,'gy'=8] {'gx'}, dimensions={1} | all-to-all | bytes 1048576 | tf_op jit(solution)/shard_map/all_to_all | solution.py:86
  118.0 19.9 %all_to_all.64 = f32[1,1,1024,128]{3,1,0,2:T(1,128)S(1)} all-to-all(f32[1,1,1024,128]{3,1,0,2:T(1,128)S(1)} %bitcast.53), channel_id=1, replica_groups=mesh['member'=4,'gx'=16,'gy'=8] {'gx'}, dimensions={2} | all-to-all | bytes 1048576 | tf_op jit(solution)/shard_map/all_to_all | solution.py:83
  139.6 1.9 collective-permute-start.1
  141.5 3.6 %collective-permute-start = (f32[1,16,1,128]{3,1,2,0:T(8,128)S(1)}, f32[1,16,1,128]{3,1,2,0:T(8,128)S(1)}, u32[]{:S(2)}, u32[]{:S(2)}) collective-permute-start(f32[1,16,1,128]{3,1,2,0:T(8,128)S(1)} %get-tuple-element.7), channel_id=1, source_target_pairs={{0,8},{8,16},{16,24},{24,32},{32,40},{40,48},{48,56},{56,64},{64,7... | collective-permute-start | bytes 24584 | tf_op jit(solution)/shard_map/ppermute | solution.py:12
  146.0 3.5 %copy.52 = f32[1,16,64,128]{1,3,2,0:T(8,128)} copy(f32[1,16,64,128]{3,2,1,0:T(8,128)} %add.66) | data formatting | bytes 1048576 | tf_op jit(solution)/shard_map/add | solution.py:98
  149.6 6.2 %gather_fusion.1 = f32[1024,16]{1,0:T(8,128)} fusion(f32[16,8192]{0,1:T(8,128)} %bitcast.51, s32[1024]{0:T(1024)S(1)} %broadcast_clamp_fusion), kind=kCustom, calls=%fused_computation.1 | custom fusion | bytes 135168 | tf_op jit(solution)/shard_map/gather | solution.py:73
  158.2 2.2 collective-permute-start.2
  163.2 8.7 %scatter_custom_fusion.2 = f32[16,8192]{0,1:T(8,128)} fusion(s32[1024]{0:T(1024)S(1)} %fusion.14, f32[]{:T(128)} %constant.6.clone.1, f32[1024,16]{1,0:T(8,128)S(1)} %reshape.142, f32[1024]{0:T(1024)S(1)} %multiply_reduce_fusion), kind=kCustom, calls=%fused_computation.10 | custom fusion | flops 32768 | bytes 1052676 | tf_op jit(solution)/shard_map/scatter-add | solution.py:69
  172.0 5.8 %sub.36 = f32[16,8192]{0,1:T(8,128)} subtract(f32[16,8192]{0,1:T(8,128)} %scatter_custom_fusion, f32[16,8192]{0,1:T(8,128)} %scatter_custom_fusion.2) | non-fusion elementwise | flops 131072 | bytes 1572864 | tf_op jit(solution)/shard_map/sub | solution.py:97
  177.8 3.5 %copy.64 = f32[1,16,64,128]{3,1,2,0:T(8,128)} copy(f32[1,16,64,128]{1,3,2,0:T(8,128)} %bitcast.45) | data formatting | bytes 1048576 | tf_op jit(solution)/shard_map/sub | solution.py:97
  182.7 1.9 select_maximum_fusion
  186.1 20.8 %all_to_all.65 = f32[1,16,64,128]{3,2,0,1:T(8,128)S(1)} all-to-all(f32[1,16,64,128]{3,2,0,1:T(8,128)S(1)} %copy.65), channel_id=1, replica_groups=mesh['member'=4,'gx'=16,'gy'=8] {'gx'}, dimensions={1} | all-to-all | bytes 1048576 | tf_op jit(solution)/shard_map/all_to_all | solution.py:86
  208.4 20.0 %all_to_all.66 = f32[1,1,1024,128]{3,1,0,2:T(1,128)S(1)} all-to-all(f32[1,1,1024,128]{3,1,0,2:T(1,128)S(1)} %bitcast.54), channel_id=1, replica_groups=mesh['member'=4,'gx'=16,'gy'=8] {'gx'}, dimensions={2} | all-to-all | bytes 1048576 | tf_op jit(solution)/shard_map/all_to_all | solution.py:83
  (64 shorter events, 22.5 us)
Async XLA Ops:
  6.5 110.0 %copy-start = (f32[1,4,256,256]{3,2,1,0:T(8,128)S(1)}, f32[1,4,256,256]{3,2,1,0:T(8,128)}, u32[]{:S(2)}) copy-start(f32[1,4,256,256]{3,2,1,0:T(8,128)} %param.13) | copy-start | bytes 3145732
  6.5 62.9 %reduce-scatter.2.cloned.1.call-start = ((), (), s32[]{:S(2)}) async-start(), calls=%async_computation.7 | async-start | bytes 2621440 | tf_op jit(solution)/shard_map/reduce_scatter | solution.py:26
  7.5 2.8 %copy-start.8 = (s32[512]{0:T(512)S(1)}, s32[512]{0:T(512)}, u32[]{:S(2)}) copy-start(s32[512]{0:T(512)} %param.17) | copy-start | bytes 6148
  7.5 2.8 %copy-start.7 = (s32[512,1]{0,1:T(1,128)S(1)}, s32[512,1]{0,1:T(1,128)}, u32[]{:S(2)}) copy-start(s32[512,1]{0,1:T(1,128)} %param.16) | copy-start | bytes 6148
  7.5 3.1 %copy-start.10 = (f32[1,512]{1,0:T(1,128)S(1)}, f32[1,512]{1,0:T(1,128)}, u32[]{:S(2)}) copy-start(f32[1,512]{1,0:T(1,128)} %param.15) | copy-start | bytes 6148
  10.2 20.6 %copy-start.9 = (f32[16,512]{1,0:T(8,128)S(1)}, f32[16,512]{1,0:T(8,128)}, u32[]{:S(2)}) copy-start(f32[16,512]{1,0:T(8,128)} %param.14) | copy-start | bytes 98308
  12.4 29.6 %all-to-all-start = ((f32[128,1,16]{2,1,0:T(1,128)}), f32[128,1,16]{2,1,0:T(1,128)S(1)}, u32[]{:S(2)}, u32[]{:S(2)}) async-start(f32[128,1,16]{2,1,0:T(1,128)} %bitcast.4), calls=%async_computation.1 | async-start | bytes 131072 | tf_op jit(solution)/shard_map/all_to_all | solution.py:54
  42.1 17.7 %all-to-all-start.1 = ((f32[128,1,128]{2,1,0:T(1,128)}), f32[128,1,128]{2,1,0:T(1,128)S(1)}, u32[]{:S(2)}, u32[]{:S(2)}) async-start(f32[128,1,128]{2,1,0:T(1,128)} %bitcast.5), calls=%async_computation.2 | async-start | bytes 131072 | tf_op jit(solution)/shard_map/all_to_all | solution.py:47
  117.8 27.4 %copy-start.2 = (f32[1,16,64,128]{3,2,1,0:T(8,128)S(1)}, f32[1,16,64,128]{3,2,1,0:T(8,128)}, u32[]{:S(2)}) copy-start(f32[1,16,64,128]{3,2,1,0:T(8,128)} %reduce-scatter.2.cloned.1.call-done) | copy-start | bytes 1572868
  139.6 16.2 %collective-permute-start.1 = (f32[1,16,1,128]{3,1,2,0:T(8,128)S(1)}, f32[1,16,1,128]{3,1,2,0:T(8,128)S(1)}, u32[]{:S(2)}, u32[]{:S(2)}) collective-permute-start(f32[1,16,1,128]{3,1,2,0:T(8,128)S(1)} %get-tuple-element.8), channel_id=1, source_target_pairs={{8,0},{16,8},{24,16},{32,24},{40,32},{48,40},{56,48},{64,56},{72,6... | collective-permute-start | bytes 24584 | tf_op jit(solution)/shard_map/ppermute | solution.py:15
  141.5 14.3 %collective-permute-start = (f32[1,16,1,128]{3,1,2,0:T(8,128)S(1)}, f32[1,16,1,128]{3,1,2,0:T(8,128)S(1)}, u32[]{:S(2)}, u32[]{:S(2)}) collective-permute-start(f32[1,16,1,128]{3,1,2,0:T(8,128)S(1)} %get-tuple-element.7), channel_id=1, source_target_pairs={{0,8},{8,16},{16,24},{24,32},{32,40},{40,48},{48,56},{56,64},{64,7... | collective-permute-start | bytes 24584 | tf_op jit(solution)/shard_map/ppermute | solution.py:12
  158.2 23.1 %collective-permute-start.2 = (f32[1,16,66,1]{2,1,3,0:T(8,128)S(1)}, f32[1,16,66,1]{2,1,3,0:T(8,128)S(1)}, u32[]{:S(2)}, u32[]{:S(2)}) collective-permute-start(f32[1,16,66,1]{2,1,3,0:T(8,128)S(1)} %copy.58), channel_id=1, source_target_pairs={{0,1},{1,2},{2,3},{3,4},{4,5},{5,6},{6,7},{8,9},{9,10},{10,11},{11... | collective-permute-start | bytes 12680 | tf_op jit(solution)/shard_map/ppermute | solution.py:12
  160.7 21.0 %collective-permute-start.3 = (f32[1,16,66,1]{2,1,3,0:T(8,128)S(1)}, f32[1,16,66,1]{2,1,3,0:T(8,128)S(1)}, u32[]{:S(2)}, u32[]{:S(2)}) collective-permute-start(f32[1,16,66,1]{2,1,3,0:T(8,128)S(1)} %copy.59), channel_id=1, source_target_pairs={{1,0},{2,1},{3,2},{4,3},{5,4},{6,5},{7,6},{9,8},{10,9},{11,10},{12... | collective-permute-start | bytes 12680 | tf_op jit(solution)/shard_map/ppermute | solution.py:15
  181.3 3.4 %copy-start.4 = (f32[16,64,128]{2,1,0:T(8,128)S(1)}, f32[16,64,128]{2,1,0:T(8,128)}, u32[]{:S(2)}) copy-start(f32[16,64,128]{2,1,0:T(8,128)} %param.12) | copy-start | bytes 1572868
  182.7 1.9 copy-start.1
  182.7 1.9 copy-start.5
  182.7 1.9 copy-start.6
  207.0 21.4 %copy-start.3 = (f32[1,16,64,128]{3,2,1,0:T(8,128)S(1)}, f32[1,16,64,128]{3,2,1,0:T(8,128)}, u32[]{:S(2)}) copy-start(f32[1,16,64,128]{3,2,1,0:T(8,128)} %reduce-scatter.2.cloned.1.call-done) | copy-start | bytes 1572868
Sparse Core Ops, SparseCore 0:
  10.4 40.4 reduce-scatter.1
where the time goes:
time: 237 us; the launch traced here: 236 us
  blocking collectives  81.6 us (34%)
  other arithmetic  50.5 us (21%)
  starting transfers between devices  33.8 us (14%)
  local copies, waits for them, and re-layouts  32.9 us (14%)
  waiting for transfers between devices  18.7 us (8%)
  between operations  13.7 us (6%)
  matrix products  4.78 us (2%)
    all_to_all x2, blocking collectives, precondition(): lax.all_to_all(resid, 'gx', split_axis=1, concat_axis=2, tiled=True)  41.7 us
    all_to_all x2, blocking collectives, solve_lines(): return lax.all_to_all(solved, 'gx', split_axis=2, concat_axis=1, tiled=True)  39.9 us
    scatter-add x3, other arithmetic, station_sum(): flat = flat.at[:, cells].add(recv_panels * weights[None, :])  26.2 us
    all_to_all x1, starting transfers between devices, shards(): lax.all_to_all(sent_extra.reshape(tile_count, slot_cap * 2), ('gx', 'gy')...  18.4 us
    gather x2, local copies, waits for them, and re-layouts, observed(): picked = field.reshape(depth, width_x * width_y)[:, cells]  11.2 us
    all_to_all x1, waiting for transfers between devices, shards(): lax.all_to_all(sent_extra.reshape(tile_count, slot_cap * 2), ('gx', 'gy')...  9.43 us
    all_to_all x1, waiting for transfers between devices, shards(): lax.all_to_all(sent_panels.reshape(tile_count, slot_cap * depth), ('gx',...  9.28 us
    sub x2, other arithmetic, shards(): forcing - observed(prior + first)  7.06 us
  transfers between devices with their start and end apart: 7, of which 2 were waited for; matrix products, arithmetic and copies ran while one was open for 19% of the time, Pallas kernels for 0%

commit v1 on v0

v1 whole, which is shorter than its diff:
```python
import functools

import jax
import jax.numpy as jnp
from jax import lax
from jax.experimental import pallas as pl
from jax.experimental.pallas import tpu as pltpu
from jax.sharding import PartitionSpec as P

F32 = jnp.float32
BF16 = jnp.bfloat16
VMEM = pl.BlockSpec(memory_space=pltpu.VMEM)
NT = (((1,), (1,)), ((), ()))
TN = (((0,), (0,)), ((), ()))


def halves(value):
    high = value.astype(BF16)
    return high, (value - high.astype(F32)).astype(BF16)


def place_kernel(slot_cap, owner_col, owner_row, panels, values, spots, sent):
    count = owner_col.shape[0]
    tiles = sent.shape[0]
    depth = panels.shape[0]
    own = lax.broadcasted_iota(jnp.int32, (count, tiles), 1) == owner_col[...]
    hits = jnp.where(own, 1.0, 0.0).astype(F32)
    later = lax.broadcasted_iota(jnp.int32, (count, count), 0)
    sooner = lax.broadcasted_iota(jnp.int32, (count, count), 1)
    earlier = jnp.where(later > sooner, 1.0, 0.0).astype(BF16)
    before = jnp.dot(earlier, hits.astype(BF16), preferred_element_type=F32)
    rank = jnp.sum(before * hits, axis=1, keepdims=True).astype(jnp.int32)
    mine = lax.broadcasted_iota(jnp.int32, (tiles, count), 0) == owner_row[...]
    hits_t = jnp.where(mine, 1.0, 0.0).astype(BF16)
    hits_t = jnp.concatenate([hits_t, hits_t], axis=1)
    lane = lax.broadcasted_iota(jnp.int32, (count, slot_cap * depth), 1)
    stacked = jnp.concatenate([panels[...]] * slot_cap, axis=0).T
    body = jnp.where(lane // depth == rank, stacked, 0.0)
    sent[:, : slot_cap * depth] = jnp.dot(
        hits_t, jnp.concatenate(halves(body), axis=0), preferred_element_type=F32
    )
    value_rows = jnp.broadcast_to(values[...], (slot_cap, count))
    spot_rows = jnp.broadcast_to(spots[...].astype(F32), (slot_cap, count))
    rest = jnp.zeros((slot_cap * (depth - 2), count), F32)
    stacked = jnp.concatenate([value_rows, spot_rows, rest], axis=0).T
    extra = jnp.where(lane % slot_cap == rank, stacked, 0.0)
    sent[:, slot_cap * depth :] = jnp.dot(
        hits_t, jnp.concatenate(halves(extra), axis=0), preferred_element_type=F32
    )


def masks(cells, width_x, width_y):
    count = cells.shape[1]
    at_x = lax.broadcasted_iota(jnp.int32, (width_x, count), 0) == cells // width_y
    at_y = lax.broadcasted_iota(jnp.int32, (width_y, count), 0) == cells % width_y
    return at_x, jnp.where(at_y, 1.0, 0.0).astype(BF16)


def project(field, panels, at_x, at_y):
    depth, width_x, width_y = field.shape
    count = at_y.shape[1]
    both = jnp.concatenate([at_y, at_y], axis=0)
    total = jnp.zeros((1, count), F32)
    for z in range(0, depth, 4):
        rows = field[z : z + 4].reshape(4 * width_x, width_y)
        seen = jnp.dot(
            jnp.concatenate(halves(rows), axis=1), both, preferred_element_type=F32
        ).reshape(4, width_x, count)
        seen = jnp.sum(jnp.where(at_x[None], seen, 0.0), axis=1)
        total = total + jnp.sum(seen * panels[z : z + 4], axis=0, keepdims=True)
    return total


def scattered(weights, panels, at_x, at_y, z):
    both = jnp.concatenate([at_y, at_y], axis=1)
    scaled = panels[z : z + 4] * weights
    high = scaled.astype(BF16).astype(F32)
    parts = [high, scaled - high]
    rows = [
        jnp.where(at_x[None], part[:, None, :], 0.0).reshape(4 * at_x.shape[0], -1).astype(BF16)
        for part in parts
    ]
    out = lax.dot_general(
        jnp.concatenate(rows, axis=1), both, NT, preferred_element_type=F32
    )
    return out.reshape(4, at_x.shape[0], at_y.shape[0])


def first_kernel(slot_cap, prior, got, resid, panels, weights, cells):
    depth, width_x, width_y = prior.shape
    tiles = got.shape[0]
    body = got[:, : slot_cap * depth].T
    extra = got[:, slot_cap * depth :].T
    for k in range(slot_cap):
        lanes = pl.ds(k * tiles, tiles)
        panels[:, lanes] = body[k * depth : (k + 1) * depth]
        weights[:, lanes] = extra[k : k + 1]
        cells[:, lanes] = extra[slot_cap + k : slot_cap + k + 1].astype(jnp.int32)
    at_x, at_y = masks(cells[...], width_x, width_y)
    left = weights[...] - project(prior, panels, at_x, at_y)
    weights[...] = left
    for z in range(0, depth, 4):
        resid[z : z + 4] = scattered(left, panels, at_x, at_y, z)


def second_kernel(first, kappa, scaling, x_low, x_high, y_low, y_high, panels, weights, cells, resid):
    depth, width_x, width_y = first.shape
    at_x, at_y = masks(cells[...], width_x, width_y)
    left = weights[...] - project(first, panels, at_x, at_y)
    column = lax.broadcasted_iota(jnp.int32, (width_x, width_y), 1)
    row = lax.broadcasted_iota(jnp.int32, (width_x, width_y), 0)
    low_y, high_y = y_low[...].T, y_high[...].T
    levels = [scaling[z] * first[z] for z in range(depth)]
    for z in range(0, depth, 4):
        summed = scattered(left, panels, at_x, at_y, z)
        for k in range(z, z + 4):
            here = levels[k]
            beside = jnp.where(row == 0, x_low[k : k + 1], pltpu.roll(here, 1, 0))
            beside = beside + jnp.where(
                row == width_x - 1, x_high[k : k + 1], pltpu.roll(here, width_x - 1, 0)
            )
            beside = beside + jnp.where(
                column == 0, low_y[:, k : k + 1], pltpu.roll(here, 1, 1)
            )
            beside = beside + jnp.where(
                column == width_y - 1, high_y[:, k : k + 1], pltpu.roll(here, width_y - 1, 1)
            )
            if k > 0:
                beside = beside + levels[k - 1]
            if k < depth - 1:
                beside = beside + levels[k + 1]
            resid[k] = summed[k - z] - (
                kappa[k] * first[k] + scaling[k] * (6.0 * here - beside)
            )


def shape(*dims, dtype=F32):
    return jax.ShapeDtypeStruct(dims, dtype)


def shards(background, mixing, kappa_sq, scaling, line_inverse, panels, values, targets, spots):
    depth, width_x, width_y = kappa_sq.shape
    member = lax.axis_index("member")
    picked = lax.dynamic_slice_in_dim(mixing, member, 1, 1)[:, 0]
    prior = lax.psum_scatter(
        picked[:, None, None, None] * background, "member", scatter_dimension=0, tiled=True
    )[0]
    tiles = lax.axis_size("gx") * lax.axis_size("gy")
    count = spots.shape[0]
    slot_cap = max(2, 2 * count // tiles)
    sent = pl.pallas_call(
        functools.partial(place_kernel, slot_cap),
        out_shape=shape(tiles, 2 * slot_cap * depth),
        in_specs=[VMEM] * 5,
        out_specs=VMEM,
    )(targets, targets.reshape(1, count), panels, values, spots.reshape(1, count))
    got = lax.all_to_all(sent, ("gx", "gy"), split_axis=0, concat_axis=0, tiled=True)
    slots = tiles * slot_cap
    resid, held, weights, cells = pl.pallas_call(
        functools.partial(first_kernel, slot_cap),
        out_shape=(
            shape(depth, width_x, width_y),
            shape(depth, slots),
            shape(1, slots),
            shape(1, slots, dtype=jnp.int32),
        ),
        in_specs=[VMEM] * 2,
        out_specs=[VMEM] * 4,
    )(prior, got)
    line = line_inverse.shape[2]

    def precondition(field):
        pencil = lax.all_to_all(field, "gx", split_axis=0, concat_axis=1, tiled=True)
        blocks = pencil.reshape(pencil.shape[0], -1, line, width_y)
        solved = jnp.einsum("zbij,zbjy->zbiy", line_inverse, blocks, precision=lax.Precision.HIGHEST)
        return lax.all_to_all(
            solved.reshape(pencil.shape), "gx", split_axis=1, concat_axis=0, tiled=True
        )

    first = precondition(resid)

    def neighbours(low_side, high_side, axis):
        forward = [(i, i + 1) for i in range(lax.axis_size(axis) - 1)]
        backward = [(i + 1, i) for i in range(lax.axis_size(axis) - 1)]
        return lax.ppermute(high_side, axis, forward), lax.ppermute(low_side, axis, backward)

    x_low, x_high = neighbours(scaling[:, 0] * first[:, 0], scaling[:, -1] * first[:, -1], "gx")
    y_low, y_high = neighbours(
        scaling[:, :, 0] * first[:, :, 0], scaling[:, :, -1] * first[:, :, -1], "gy"
    )
    again = pl.pallas_call(
        second_kernel,
        out_shape=shape(depth, width_x, width_y),
        in_specs=[VMEM] * 10,
        out_specs=VMEM,
    )(first, kappa_sq, scaling, x_low, x_high, y_low, y_high, held, weights, cells)
    return (prior + (first + precondition(again)))[None]


def solution(mesh):
    return jax.shard_map(
        shards,
        mesh=mesh,
        in_specs=(
            P("member", None, "gx", "gy"),
            P(),
            P(None, "gx", "gy"),
            P(None, "gx", "gy"),
            P("gx", None, None, None),
            P(None, ("gx", "gy")),
            P("member", ("gx", "gy")),
            P(("gx", "gy"), None),
            P(("gx", "gy")),
        ),
        out_specs=P("member", None, "gx", "gy"),
        check_vma=False,
    )
```

time: 237 us -> 176 us (0.74)
  other arithmetic: 50.5 us -> 4.15 us
  local copies, waits for them, and re-layouts: 32.9 us -> 6.54 us
  starting transfers between devices: 33.8 us -> 12.2 us
  blocking collectives: 81.6 us -> 100 us
  Pallas kernels: 0 us -> 11.1 us
  waiting for transfers between devices: 18.7 us -> 23.9 us
    scatter-add x3 -> x0, other arithmetic: 26.2 us -> none  [station_sum(): flat = flat.at[:, cells].add(recv_panels * weights[None, :])]
    all_to_all x2 -> x1, starting transfers between devices: 24.7 us -> 3.47 us  [precondition(): lax.all_to_all(solved.reshape(pencil.shape), 'gx', split_axis=1, concat_a...]
    all_to_all x4, blocking collectives: 81.6 us -> 100 us  [the longest x2 49.3 us: precondition(): lax.all_to_all(field, 'gx', split_axis=0, concat_axis=1, tiled=True)]
    sub x3 -> x0, other arithmetic: 12.9 us -> none  [the longest x2 7.06 us: shards(): forcing - observed(prior + first)]
    gather x2 -> x0, local copies, waits for them, and re-layouts: 11.2 us -> none  [observed(): picked = field.reshape(depth, width_x * width_y)[:, cells]]
    pallas_call x0 -> x3, Pallas kernels: none -> 11.1 us  [the longest x1 4.4 us: shards(): pl.pallas_call(second_kernel, out_shape=shape(depth, width_x, width_y), i...]
    sub x3 -> x0, local copies, waits for them, and re-layouts: 6.52 us -> none  [the longest x2 3.67 us: shards(): forcing - observed(prior + first)]
    reduce_scatter x1, waiting for transfers between devices: 0.01 us -> 4.65 us  [shards(): lax.psum_scatter(picked[:, None, None, None] * background, 'member', scat...]
  transfers between devices with their start and end apart: 7 -> 6, of which waited for: 2 -> 3; matrix products, arithmetic and copies ran while one was open for 19% -> 2% of each run, Pallas kernels for 0% -> 2%
where the time goes in v1:
time: 176 us; the launch traced here: 174 us
  blocking collectives  100 us (57%)
  waiting for transfers between devices  23.9 us (14%)
  between operations  13.6 us (8%)
  starting transfers between devices  12.2 us (7%)
  Pallas kernels  11.1 us (6%)
  local copies, waits for them, and re-layouts  6.54 us (4%)
  other arithmetic  4.15 us (2%)
  matrix products  2.5 us (1%)
    all_to_all x2, blocking collectives, precondition(): lax.all_to_all(field, 'gx', split_axis=0, concat_axis=1, tiled=True)  49.3 us
    all_to_all x1, blocking collectives, shards(): lax.all_to_all(sent, ('gx', 'gy'), split_axis=0, concat_axis=0, tiled=True)  30.8 us
    all_to_all x1, blocking collectives, precondition(): lax.all_to_all(solved.reshape(pencil.shape), 'gx', split_axis=1, concat_a...  20 us
    all_to_all x1, waiting for transfers between devices, precondition(): lax.all_to_all(solved.reshape(pencil.shape), 'gx', split_axis=1, concat_a...  16.1 us
    ppermute x2, starting transfers between devices, neighbours(): lax.ppermute(high_side, axis, forward)  5.05 us
    reduce_scatter x1, waiting for transfers between devices, shards(): lax.psum_scatter(picked[:, None, None, None] * background, 'member', scat...  4.65 us
    pallas_call x1, Pallas kernels, shards(): pl.pallas_call(second_kernel, out_shape=shape(depth, width_x, width_y), i...  4.4 us
    pallas_call x1, Pallas kernels, shards(): pl.pallas_call(functools.partial(first_kernel, slot_cap), out_shape=(shap...  4.04 us
  transfers between devices with their start and end apart: 6, of which 3 were waited for; matrix products, arithmetic and copies ran while one was open for 2% of the time, Pallas kernels for 2%

profile of v1, /device:TPU:1, one launch (start us, length us, event | category | flops | bytes accessed | tf_op | source)
XLA Modules:
  0.0 174.0 jit_solution(11634646387595057618)
XLA Ops:
  6.5 1.0 dynamic-slice_reduce_fusion
  7.5 2.7 %broadcast_multiply_fusion = f32[4,16,64,128]{3,2,1,0:T(8,128)} fusion(f32[16,64,128]{2,1,0:T(8,128)} %bitcast.45, f32[4]{0:T(128)S(1)} %dynamic-slice_reduce_fusion), kind=kLoop, calls=%fused_computation.4 | loop fusion | flops 524288 | bytes 2621456 | tf_op jit(solution)/shard_map/mul | solution.py:146
  10.2 0.9 copy.30.owner_col
  11.1 2.6 %shard_map.91 = f32[128,256]{1,0:T(8,128)} custom-call(s32[512,1]{1,0:T(8,128)} %copy.30.owner_col, s32[1,512]{1,0:T(1,128)} %bitcast.46, f32[16,512]{1,0:T(8,128)} %panels.1, f32[1,512]{1,0:T(1,128)} %values.1, s32[1,512]{1,0:T(1,128)} %bitcast.49), custom_call_target="tpu_custom_call" | custom-call | tf_op jit(solution)/shard_map/pallas_call | solution.py:151
  13.7 1.0 copy.31
  14.8 30.8 %all_to_all.50 = f32[128,1,256]{2,1,0:T(1,128)S(1)} all-to-all(f32[128,1,256]{2,1,0:T(1,128)S(1)} %copy.31), channel_id=1, replica_groups=mesh['member'=4,'gx'=16,'gy'=8] {'gx','gy'}, dimensions={0} | all-to-all | bytes 262144 | tf_op jit(solution)/shard_map/all_to_all | solution.py:157
  45.5 0.7 copy.50
  46.2 4.6 %reduce-scatter.2.cloned.1.call-done = f32[1,16,64,128]{3,2,1,0:T(8,128)} async-done(((f32[4,16,64,128]{3,2,1,0:T(8,128)}), f32[1,16,64,128]{3,2,1,0:T(8,128)}) %reduce-scatter.2.cloned.1.call-update) | async-done | bytes 524304 | tf_op jit(solution)/shard_map/reduce_scatter | solution.py:145
  50.8 4.0 %shard_map.92 = (f32[16,64,128]{2,1,0:T(8,128)}, f32[16,1024]{1,0:T(8,128)}, f32[1,1024]{1,0:T(1,128)}, s32[1,1024]{1,0:T(1,128)}) custom-call(f32[16,64,128]{2,1,0:T(8,128)} %bitcast.38, f32[128,256]{1,0:T(8,128)} %bitcast.43), custom_call_target="tpu_custom_call" | custom-call | tf_op jit(solution)/shard_map/pallas_call | solution.py:159
  54.9 25.3 %all_to_all.51 = f32[16,64,128]{2,1,0:T(8,128)S(1)} all-to-all(f32[16,64,128]{2,1,0:T(8,128)} %get-tuple-element.9), channel_id=1, replica_groups=mesh['member'=4,'gx'=16,'gy'=8] {'gx'}, dimensions={0} | all-to-all | bytes 1048576 | tf_op jit(solution)/shard_map/all_to_all | solution.py:173
  80.2 1.2 convolution_bitcast_fusion.1
  81.4 1.0 copy.33
  82.4 3.5 %all-to-all-start.2 = ((f32[1,1024,128]{2,0,1:T(1,128)}), f32[1,1024,128]{2,0,1:T(1,128)S(1)}, u32[]{:S(2)}, u32[]{:S(2)}) async-start(f32[1,1024,128]{2,0,1:T(1,128)} %bitcast.9), calls=%async_computation.3 | async-start | bytes 1048576 | tf_op jit(solution)/shard_map/all_to_all | solution.py:176
  86.6 16.1 %all-to-all-done.2 = f32[1,1024,128]{2,0,1:T(1,128)S(1)} async-done(((f32[1,1024,128]{2,0,1:T(1,128)}), f32[1,1024,128]{2,0,1:T(1,128)S(1)}, u32[]{:S(2)}, u32[]{:S(2)}) %all-to-all-start.2) | async-done | bytes 524320 | tf_op jit(solution)/shard_map/all_to_all | solution.py:176
  103.1 3.1 %collective-permute-start.2 = (f32[16,64]{1,0:T(8,128)S(1)}, f32[16,64]{1,0:T(8,128)S(1)}, u32[]{:S(2)}, u32[]{:S(2)}) collective-permute-start(f32[16,64]{1,0:T(8,128)S(1)} %multiply_bitcast_fusion.1), channel_id=1, source_target_pairs={{0,1},{1,2},{2,3},{3,4},{4,5},{5,6},{6,7},{8,9},{9,10},{10,11},{11... | collective-permute-start | bytes 12296 | tf_op jit(solution)/shard_map/ppermute | solution.py:185
  106.4 1.9 %collective-permute-start = (f32[16,128]{1,0:T(8,128)S(1)}, f32[16,128]{1,0:T(8,128)S(1)}, u32[]{:S(2)}, u32[]{:S(2)}) collective-permute-start(f32[16,128]{1,0:T(8,128)S(1)} %bitcast.48), channel_id=1, source_target_pairs={{0,8},{8,16},{16,24},{24,32},{32,40},{40,48},{48,56},{56,64},{64,7... | collective-permute-start | bytes 24584 | tf_op jit(solution)/shard_map/ppermute | solution.py:185
  108.3 2.4 %collective-permute-start.1 = (f32[16,128]{1,0:T(8,128)S(1)}, f32[16,128]{1,0:T(8,128)S(1)}, u32[]{:S(2)}, u32[]{:S(2)}) collective-permute-start(f32[16,128]{1,0:T(8,128)S(1)} %bitcast.47), channel_id=1, source_target_pairs={{8,0},{16,8},{24,16},{32,24},{40,32},{48,40},{56,48},{64,56},{72,6... | collective-permute-start | bytes 24584 | tf_op jit(solution)/shard_map/ppermute | solution.py:185
  110.8 1.3 collective-permute-start.3
  112.1 3.2 %collective-permute-done.3.y_high = f32[16,64]{1,0:T(8,128)S(1)} collective-permute-done((f32[16,64]{1,0:T(8,128)S(1)}, f32[16,64]{1,0:T(8,128)S(1)}, u32[]{:S(2)}, u32[]{:S(2)}) %collective-permute-start.3) | collective-permute-done | bytes 4128 | tf_op jit(solution)/shard_map/ppermute | solution.py:185
  115.9 4.4 %shard_map.93 = f32[16,64,128]{2,1,0:T(8,128)} custom-call(f32[16,64,128]{2,1,0:T(8,128)} %bitcast.37, f32[16,64,128]{2,1,0:T(8,128)} %kappa.1, f32[16,64,128]{2,1,0:T(8,128)} %scaling.1, f32[16,128]{1,0:T(8,128)} %copy-done.6, f32[16,128]{1,0:T(8,128)} %copy-done.7, f32[16,64]{1,0:T(8,128)} %copy-done.5, f32[16,64]{1,0:T(8,128)} %copy-done.8, ...), custom_call_target="tpu_custom_call" | custom-call | tf_op jit(solution)/shard_map/pallas_call | solution.py:191
  120.3 23.9 %all_to_all.52 = f32[16,64,128]{2,1,0:T(8,128)S(1)} all-to-all(f32[16,64,128]{2,1,0:T(8,128)} %shard_map.93), channel_id=1, replica_groups=mesh['member'=4,'gx'=16,'gy'=8] {'gx'}, dimensions={0} | all-to-all | bytes 1048576 | tf_op jit(solution)/shard_map/all_to_all | solution.py:173
  144.2 1.3 convolution_bitcast_fusion
  145.7 20.0 %all_to_all.53 = f32[1,1024,128]{2,0,1:T(1,128)S(1)} all-to-all(f32[1,1024,128]{2,0,1:T(1,128)S(1)} %bitcast.40), channel_id=1, replica_groups=mesh['member'=4,'gx'=16,'gy'=8] {'gx'}, dimensions={1} | all-to-all | bytes 1048576 | tf_op jit(solution)/shard_map/all_to_all | solution.py:176
  166.3 0.9 add.25
  (36 shorter events, 2.6 us)
Async XLA Ops:
  6.5 73.7 %copy-start = (f32[1,4,256,256]{3,2,1,0:T(8,128)S(1)}, f32[1,4,256,256]{3,2,1,0:T(8,128)}, u32[]{:S(2)}) copy-start(f32[1,4,256,256]{3,2,1,0:T(8,128)} %param.13) | copy-start | bytes 3145732
  6.5 44.3 %reduce-scatter.2.cloned.1.call-start = ((), (), s32[]{:S(2)}) async-start(), calls=%async_computation.6 | async-start | bytes 2621440 | tf_op jit(solution)/shard_map/reduce_scatter | solution.py:145
  7.5 2.7 %copy-start.9 = (s32[512,1]{0,1:T(1,128)S(1)}, s32[512,1]{0,1:T(1,128)}, u32[]{:S(2)}) copy-start(s32[512,1]{0,1:T(1,128)} %param.16) | copy-start | bytes 6148
  80.2 5.7 %copy-start.3 = (f32[16,64,128]{2,1,0:T(8,128)S(1)}, f32[16,64,128]{2,1,0:T(8,128)}, u32[]{:S(2)}) copy-start(f32[16,64,128]{2,1,0:T(8,128)} %scaling.1) | copy-start | bytes 1572868
  82.4 20.2 %all-to-all-start.2 = ((f32[1,1024,128]{2,0,1:T(1,128)}), f32[1,1024,128]{2,0,1:T(1,128)S(1)}, u32[]{:S(2)}, u32[]{:S(2)}) async-start(f32[1,1024,128]{2,0,1:T(1,128)} %bitcast.9), calls=%async_computation.3 | async-start | bytes 1048576 | tf_op jit(solution)/shard_map/all_to_all | solution.py:176
  102.6 12.7 %copy-start.1 = (f32[1,1024,128]{2,0,1:T(1,128)}, f32[1,1024,128]{2,0,1:T(1,128)S(1)}, u32[]{:S(2)}) copy-start(f32[1,1024,128]{2,0,1:T(1,128)S(1)} %all-to-all-done.2) | copy-start | bytes 1572868
  103.1 9.0 %collective-permute-start.2 = (f32[16,64]{1,0:T(8,128)S(1)}, f32[16,64]{1,0:T(8,128)S(1)}, u32[]{:S(2)}, u32[]{:S(2)}) collective-permute-start(f32[16,64]{1,0:T(8,128)S(1)} %multiply_bitcast_fusion.1), channel_id=1, source_target_pairs={{0,1},{1,2},{2,3},{3,4},{4,5},{5,6},{6,7},{8,9},{9,10},{10,11},{11... | collective-permute-start | bytes 12296 | tf_op jit(solution)/shard_map/ppermute | solution.py:185
  106.4 8.9 %collective-permute-start = (f32[16,128]{1,0:T(8,128)S(1)}, f32[16,128]{1,0:T(8,128)S(1)}, u32[]{:S(2)}, u32[]{:S(2)}) collective-permute-start(f32[16,128]{1,0:T(8,128)S(1)} %bitcast.48), channel_id=1, source_target_pairs={{0,8},{8,16},{16,24},{24,32},{32,40},{40,48},{48,56},{56,64},{64,7... | collective-permute-start | bytes 24584 | tf_op jit(solution)/shard_map/ppermute | solution.py:185
  108.3 7.0 %collective-permute-start.1 = (f32[16,128]{1,0:T(8,128)S(1)}, f32[16,128]{1,0:T(8,128)S(1)}, u32[]{:S(2)}, u32[]{:S(2)}) collective-permute-start(f32[16,128]{1,0:T(8,128)S(1)} %bitcast.47), channel_id=1, source_target_pairs={{8,0},{16,8},{24,16},{32,24},{40,32},{48,40},{56,48},{64,56},{72,6... | collective-permute-start | bytes 24584 | tf_op jit(solution)/shard_map/ppermute | solution.py:185
  110.8 4.5 %collective-permute-start.3 = (f32[16,64]{1,0:T(8,128)S(1)}, f32[16,64]{1,0:T(8,128)S(1)}, u32[]{:S(2)}, u32[]{:S(2)}) collective-permute-start(f32[16,64]{1,0:T(8,128)S(1)} %multiply_bitcast_fusion), channel_id=1, source_target_pairs={{1,0},{2,1},{3,2},{4,3},{5,4},{6,5},{7,6},{9,8},{10,9},{11,10},{12... | collective-permute-start | bytes 12296 | tf_op jit(solution)/shard_map/ppermute | solution.py:185
  112.1 3.3 %copy-start.5 = (f32[16,64]{1,0:T(8,128)}, f32[16,64]{1,0:T(8,128)S(1)}, u32[]{:S(2)}) copy-start(f32[16,64]{1,0:T(8,128)S(1)} %collective-permute-done.2.y_low) | copy-start | bytes 12292
  115.3 0.6 copy-start.8
  115.3 0.6 copy-start.6
  115.3 0.6 copy-start.7
  144.2 21.5 %copy-start.2 = (f32[1,1024,128]{2,0,1:T(1,128)S(1)}, f32[1,1024,128]{2,0,1:T(1,128)}, u32[]{:S(2)}) copy-start(f32[1,1024,128]{2,0,1:T(1,128)} %copy-done.1) | copy-start | bytes 1572868
  145.5 20.7 %copy-start.4 = (f32[1,16,64,128]{3,2,1,0:T(8,128)S(1)}, f32[1,16,64,128]{3,2,1,0:T(8,128)}, u32[]{:S(2)}) copy-start(f32[1,16,64,128]{3,2,1,0:T(8,128)} %reduce-scatter.2.cloned.1.call-done) | copy-start | bytes 1572868
Sparse Core Ops, SparseCore 0:
  10.4 40.4 reduce-scatter.1

commit v2 on v1

v2 whole, which is shorter than its diff:
```python
import functools

import jax
import jax.numpy as jnp
from jax import lax
from jax.experimental import pallas as pl
from jax.experimental.pallas import tpu as pltpu
from jax.sharding import PartitionSpec as P

F32 = jnp.float32
BF16 = jnp.bfloat16
VMEM = pl.BlockSpec(memory_space=pltpu.VMEM)
ANY = pl.BlockSpec(memory_space=pl.ANY)
MESH = pl.DeviceIdType.MESH
NT = (((1,), (1,)), ((), ()))
TN = (((0,), (0,)), ((), ()))


def halves(value):
    high = value.astype(BF16)
    return high, (value - high.astype(F32)).astype(BF16)


def place_kernel(slot_cap, grid_y, owner_col, owner_row, panels, values, spots, sent):
    count = owner_col.shape[0]
    tiles = sent.shape[0]
    depth = panels.shape[0]
    grid_x = tiles // grid_y
    column = (owner_col[...] % grid_y) * grid_x + owner_col[...] // grid_y
    across = (owner_row[...] % grid_y) * grid_x + owner_row[...] // grid_y
    own = lax.broadcasted_iota(jnp.int32, (count, tiles), 1) == column
    hits = jnp.where(own, 1.0, 0.0).astype(F32)
    later = lax.broadcasted_iota(jnp.int32, (count, count), 0)
    sooner = lax.broadcasted_iota(jnp.int32, (count, count), 1)
    earlier = jnp.where(later > sooner, 1.0, 0.0).astype(BF16)
    before = jnp.dot(earlier, hits.astype(BF16), preferred_element_type=F32)
    rank = jnp.sum(before * hits, axis=1, keepdims=True).astype(jnp.int32)
    mine = lax.broadcasted_iota(jnp.int32, (tiles, count), 0) == across
    hits_t = jnp.where(mine, 1.0, 0.0).astype(BF16)
    hits_t = jnp.concatenate([hits_t, hits_t], axis=1)
    lane = lax.broadcasted_iota(jnp.int32, (count, slot_cap * depth), 1)
    stacked = jnp.concatenate([panels[...]] * slot_cap, axis=0).T
    body = jnp.where(lane // depth == rank, stacked, 0.0)
    sent[:, 0, :] = jnp.dot(
        hits_t, jnp.concatenate(halves(body), axis=0), preferred_element_type=F32
    )
    value_rows = jnp.broadcast_to(values[...], (slot_cap, count))
    spot_rows = jnp.broadcast_to(spots[...].astype(F32), (slot_cap, count))
    rest = jnp.zeros((slot_cap * (depth - 2), count), F32)
    stacked = jnp.concatenate([value_rows, spot_rows, rest], axis=0).T
    extra = jnp.where(lane % slot_cap == rank, stacked, 0.0)
    sent[:, 1, :] = jnp.dot(
        hits_t, jnp.concatenate(halves(extra), axis=0), preferred_element_type=F32
    )


def masks(cells, width_x, width_y):
    count = cells.shape[1]
    at_x = lax.broadcasted_iota(jnp.int32, (width_x, count), 0) == cells // width_y
    at_y = lax.broadcasted_iota(jnp.int32, (width_y, count), 0) == cells % width_y
    return at_x, jnp.where(at_y, 1.0, 0.0).astype(BF16)


def project(field, panels, at_x, at_y):
    depth, width_x, width_y = field.shape
    count = at_y.shape[1]
    both = jnp.concatenate([at_y, at_y], axis=0)
    total = jnp.zeros((1, count), F32)
    for z in range(0, depth, 4):
        rows = field[z : z + 4].reshape(4 * width_x, width_y)
        seen = jnp.dot(
            jnp.concatenate(halves(rows), axis=1), both, preferred_element_type=F32
        ).reshape(4, width_x, count)
        seen = jnp.sum(jnp.where(at_x[None], seen, 0.0), axis=1)
        total = total + jnp.sum(seen * panels[z : z + 4], axis=0, keepdims=True)
    return total


def scattered(weights, panels, at_x, at_y, z):
    both = jnp.concatenate([at_y, at_y], axis=1)
    scaled = panels[z : z + 4] * weights
    high = scaled.astype(BF16).astype(F32)
    parts = [high, scaled - high]
    rows = [
        jnp.where(at_x[None], part[:, None, :], 0.0).reshape(4 * at_x.shape[0], -1).astype(BF16)
        for part in parts
    ]
    out = lax.dot_general(
        jnp.concatenate(rows, axis=1), both, NT, preferred_element_type=F32
    )
    return out.reshape(4, at_x.shape[0], at_y.shape[0])


def greet(devices):
    barrier = pltpu.get_barrier_semaphore()
    for device in devices:
        pl.semaphore_signal(barrier, inc=1, device_id=device, device_id_type=MESH)
    pl.semaphore_wait(barrier, len(devices))


def remote(source, target, sends, receives, device):
    return pltpu.make_async_remote_copy(
        src_ref=source,
        dst_ref=target,
        send_sem=sends,
        recv_sem=receives,
        device_id=device,
        device_id_type=MESH,
    )


def spread_kernel(
    members, grid_x, grid_y, background, line, sent, others, lines, got, mid,
    own_send, own_recv, relay_send, relay_recv, line_send, line_recv, pass_send, pass_recv,
    y_send, y_recv, x_send, x_recv, here,
):
    m, g, h = lax.axis_index("member"), lax.axis_index("gx"), lax.axis_index("gy")
    right = {"member": (m + 1) % members}
    left = {"member": (m + members - 1) % members}
    along_x = [{"gx": (g + d) % grid_x} for d in range(1, grid_x)]
    along_y = [{"gy": (h + d) % grid_y} for d in range(1, grid_y)]
    mate = {"gy": h + 1 - 2 * (h % 2)}
    greet([right, left] + along_x + along_y)

    half = background.shape[0] // 2
    low, high = pl.ds(0, half), pl.ds(half, half)
    wide = lines.shape[1]
    part = wide // 2
    quads = line.shape[1] // wide
    start = pl.multiple_of((h % 2) * part, part)

    stations = [
        remote(sent.at[(h + d) % grid_y], mid.at[h], y_send.at[d - 1], y_recv.at[d - 1], along_y[d - 1])
        for d in range(1, grid_y)
    ]
    for copy in stations:
        copy.start()
    mine = pltpu.make_async_copy(sent.at[h], mid.at[h], here.at[0])
    mine.start()
    own = [
        remote(background.at[piece], others.at[slot, piece], own_send.at[k], own_recv.at[k], device)
        for k, (piece, slot, device) in enumerate(
            [(low, 0, right), (high, 1, left), (high, 0, right), (low, 1, left)]
        )
    ]
    for copy in own:
        copy.start()
    pieces = []
    for d in range(1, grid_x):
        to = (g + d) % grid_x
        rows = pl.ds(pl.multiple_of((to % quads) * wide + start, part), part)
        pieces.append(
            remote(
                line.at[to // quads, rows],
                lines.at[g, pl.ds(start, part)],
                line_send.at[d - 1],
                line_recv.at[d - 1],
                along_x[d - 1],
            )
        )
        pieces[-1].start()
    mine_rows = pl.ds(pl.multiple_of((g % quads) * wide, wide), wide)
    level = pltpu.make_async_copy(line.at[g // quads, mine_rows], lines.at[g], here.at[1])
    level.start()

    mine.wait()
    for copy in stations:
        copy.wait_recv()
    second = [
        remote(mid.at[:, (g + d) % grid_x], got.at[g], x_send.at[d - 1], x_recv.at[d - 1], along_x[d - 1])
        for d in range(1, grid_x)
    ]
    for copy in second:
        copy.start()
    last = pltpu.make_async_copy(mid.at[:, g], got.at[g], here.at[2])
    last.start()

    own[0].wait_recv()
    relay = [
        remote(others.at[0, low], others.at[2, low], relay_send.at[0], relay_recv.at[0], right),
        remote(others.at[1, high], others.at[2, high], relay_send.at[1], relay_recv.at[1], left),
    ]
    relay[0].start()
    own[1].wait_recv()
    relay[1].start()

    passed = []
    for d in range(1, grid_x):
        pieces[d - 1].wait_recv()
        came = lines.at[(g + grid_x - d) % grid_x, pl.ds(start, part)]
        passed.append(remote(came, came, pass_send.at[d - 1], pass_recv.at[d - 1], mate))
        passed[-1].start()

    level.wait()
    last.wait()
    for copy in second + passed + relay:
        copy.wait()
    for copy in own[2:]:
        copy.wait()
    for copy in own[:2] + stations + pieces:
        copy.wait_send()


def gather_kernel(field, whole, far_send, far_recv, near_send, near_recv, pass_send, pass_recv):
    g = lax.axis_index("gx")
    flip = 2 - 4 * ((g // 2) % 2)
    near = {"gx": g + 1 - 2 * (g % 2)}
    far = {"gx": g + flip}
    greet([near, far])
    chunks = far_send.shape[0]
    size = field.shape[0] // chunks
    place, other = g % 4, (g + flip) % 4
    spans = [pl.ds(c * size, size) for c in range(chunks)]
    outs, ins, passed = [], [], []
    for c, span in enumerate(spans):
        outs.append(remote(field.at[span], whole.at[place, span], far_send.at[c], far_recv.at[c], far))
        outs[-1].start()
    for c, span in enumerate(spans):
        ins.append(remote(field.at[span], whole.at[place, span], near_send.at[c], near_recv.at[c], near))
        ins[-1].start()
    for c, span in enumerate(spans):
        outs[c].wait_recv()
        passed.append(
            remote(whole.at[other, span], whole.at[other, span], pass_send.at[c], pass_recv.at[c], near)
        )
        passed[-1].start()
    for copy in ins + passed:
        copy.wait()
    for copy in outs:
        copy.wait_send()


def rim_kernel(grid_x, grid_y, x_rim, y_rim, x_low, x_high, y_low, y_high, sends, receives):
    g, h = lax.axis_index("gx"), lax.axis_index("gy")
    up_x, down_x = {"gx": (g + 1) % grid_x}, {"gx": (g + grid_x - 1) % grid_x}
    up_y, down_y = {"gy": (h + 1) % grid_y}, {"gy": (h + grid_y - 1) % grid_y}
    greet([up_x, down_x, up_y, down_y])
    copies = [
        remote(source, target, sends.at[k], receives.at[k], device)
        for k, (source, target, device) in enumerate(
            [
                (x_rim, x_low, up_x),
                (x_rim, x_high, down_x),
                (y_rim, y_low, up_y),
                (y_rim, y_high, down_y),
            ]
        )
    ]
    for copy in copies:
        copy.start()
    for copy in copies:
        copy.wait()


def first_kernel(slot_cap, members, mixing, background, others, got, prior, resid, panels, weights, cells):
    depth, width_x, width_y = background.shape
    tiles = got.shape[0]
    m = lax.axis_index("member")
    prior[...] = (
        mixing[m, m] * background[...]
        + mixing[m, (m + members - 1) % members] * others[0]
        + mixing[m, (m + 1) % members] * others[1]
        + mixing[m, (m + 2) % members] * others[2]
    )
    body = got[:, 0, :].T
    extra = got[:, 1, :].T
    for k in range(slot_cap):
        lanes = pl.ds(k * tiles, tiles)
        panels[:, lanes] = body[k * depth : (k + 1) * depth]
        weights[:, lanes] = extra[k : k + 1]
        cells[:, lanes] = extra[slot_cap + k : slot_cap + k + 1].astype(jnp.int32)
    at_x, at_y = masks(cells[...], width_x, width_y)
    left = weights[...] - project(prior, panels, at_x, at_y)
    weights[...] = left
    for z in range(0, depth, 4):
        resid[z : z + 4] = scattered(left, panels, at_x, at_y, z)


def solved_level(lines, field, whole, z):
    place = lax.axis_index("gx") % 4
    rows = jnp.concatenate(
        [jnp.where(place == p, field[z], whole[p, z]) for p in range(4)], axis=0
    )
    left = jnp.concatenate(halves(lines[z]), axis=0)
    out = jnp.dot(left, jnp.concatenate(halves(rows), axis=1), preferred_element_type=F32)
    width_x, width_y = field.shape[1:]
    return out[:width_x, :width_y] + (out[width_x:, :width_y] + out[:width_x, width_y:])


def solve_kernel(lines, field, whole, scaling, first, x_rim, y_rim):
    depth, width_x, width_y = field.shape
    lane = lax.broadcasted_iota(jnp.int32, (width_x, width_y), 1)
    rims = jnp.zeros((width_x, width_y), F32)
    for z in range(depth):
        level = solved_level(lines, field, whole, z)
        first[z] = level
        scaled = scaling[z] * level
        x_rim[z : z + 1] = scaled[:1]
        x_rim[depth + z : depth + z + 1] = scaled[width_x - 1 :]
        rims = jnp.where(lane == z, scaled[:, :1], rims)
        rims = jnp.where(lane == depth + z, scaled[:, width_y - 1 :], rims)
    y_rim[...] = rims


def finish_kernel(lines, field, whole, prior, first, out):
    for z in range(field.shape[0]):
        out[z] = prior[z] + (first[z] + solved_level(lines, field, whole, z))


def second_kernel(
    grid_x, grid_y, first, kappa, scaling, x_low, x_high, y_low, y_high, panels, weights, cells, resid
):
    depth, width_x, width_y = first.shape
    g, h = lax.axis_index("gx"), lax.axis_index("gy")
    at_x, at_y = masks(cells[...], width_x, width_y)
    left = weights[...] - project(first, panels, at_x, at_y)
    column = lax.broadcasted_iota(jnp.int32, (width_x, width_y), 1)
    row = lax.broadcasted_iota(jnp.int32, (width_x, width_y), 0)
    low_x = jnp.where(g > 0, x_low[...], 0.0)
    high_x = jnp.where(g < grid_x - 1, x_high[...], 0.0)
    low_y = jnp.where(h > 0, y_low[...], 0.0)
    high_y = jnp.where(h < grid_y - 1, y_high[...], 0.0)
    levels = [scaling[z] * first[z] for z in range(depth)]
    for z in range(0, depth, 4):
        summed = scattered(left, panels, at_x, at_y, z)
        for k in range(z, z + 4):
            here = levels[k]
            beside = jnp.where(row == 0, low_x[depth + k : depth + k + 1], pltpu.roll(here, 1, 0))
            beside = beside + jnp.where(
                row == width_x - 1, high_x[k : k + 1], pltpu.roll(here, width_x - 1, 0)
            )
            beside = beside + jnp.where(
                column == 0, low_y[:, depth + k : depth + k + 1], pltpu.roll(here, 1, 1)
            )
            beside = beside + jnp.where(
                column == width_y - 1, high_y[:, k : k + 1], pltpu.roll(here, width_y - 1, 1)
            )
            if k > 0:
                beside = beside + levels[k - 1]
            if k < depth - 1:
                beside = beside + levels[k + 1]
            resid[k] = summed[k - z] - (
                kappa[k] * first[k] + scaling[k] * (6.0 * here - beside)
            )


def shape(*dims, dtype=F32):
    return jax.ShapeDtypeStruct(dims, dtype)


def dma(count):
    return pltpu.SemaphoreType.DMA((count,))


def shards(background, mixing, kappa_sq, scaling, line_inverse, panels, values, targets, spots):
    depth, width_x, width_y = kappa_sq.shape
    members = lax.axis_size("member")
    grid_x, grid_y = lax.axis_size("gx"), lax.axis_size("gy")
    tiles = grid_x * grid_y
    count = spots.shape[0]
    slot_cap = max(2, 2 * count // tiles)
    field = shape(depth, width_x, width_y)
    line = line_inverse.shape[2]
    background, line_inverse = background[0], line_inverse[0]
    sent = pl.pallas_call(
        functools.partial(place_kernel, slot_cap, grid_y),
        out_shape=shape(tiles, 2, slot_cap * depth),
        in_specs=[VMEM] * 5,
        out_specs=VMEM,
    )(targets, targets.reshape(1, count), panels, values, spots.reshape(1, count))
    pair = (2, slot_cap * depth)
    others, lines, got = pl.pallas_call(
        functools.partial(spread_kernel, members, grid_x, grid_y),
        out_shape=(
            shape(members - 1, depth, width_x, width_y),
            shape(depth, width_x, line),
            shape(grid_x, grid_y, *pair),
        ),
        in_specs=[ANY, ANY, VMEM],
        out_specs=(ANY, ANY, VMEM),
        scratch_shapes=[
            pltpu.VMEM((grid_y, grid_x, *pair), F32),
            dma(4), dma(4), dma(2), dma(2),
            dma(grid_x - 1), dma(grid_x - 1), dma(grid_x - 1), dma(grid_x - 1),
            dma(grid_y - 1), dma(grid_y - 1), dma(grid_x - 1), dma(grid_x - 1),
            dma(3),
        ],
        compiler_params=pltpu.CompilerParams(collective_id=0, has_side_effects=True),
    )(background, line_inverse, sent.reshape(grid_y, grid_x, *pair))
    slots = tiles * slot_cap
    prior, resid, held, weights, cells = pl.pallas_call(
        functools.partial(first_kernel, slot_cap, members),
        out_shape=(
            field,
            field,
            shape(depth, slots),
            shape(1, slots),
            shape(1, slots, dtype=jnp.int32),
        ),
        in_specs=[pl.BlockSpec(memory_space=pltpu.SMEM)] + [VMEM] * 3,
        out_specs=[VMEM] * 5,
    )(mixing, background, others, got.reshape(tiles, *pair))

    def gathered(piece):
        return pl.pallas_call(
            gather_kernel,
            out_shape=shape(4, depth, width_x, width_y),
            in_specs=[ANY],
            out_specs=ANY,
            scratch_shapes=[dma(4)] * 6,
            compiler_params=pltpu.CompilerParams(collective_id=1, has_side_effects=True),
        )(piece)

    first, x_rim, y_rim = pl.pallas_call(
        solve_kernel,
        out_shape=(field, shape(2 * depth, width_y), shape(width_x, width_y)),
        in_specs=[VMEM] * 4,
        out_specs=[VMEM] * 3,
    )(lines, resid, gathered(resid), scaling)
    rims = pl.pallas_call(
        functools.partial(rim_kernel, grid_x, grid_y),
        out_shape=[shape(2 * depth, width_y)] * 2 + [shape(width_x, width_y)] * 2,
        in_specs=[VMEM] * 2,
        out_specs=[VMEM] * 4,
        scratch_shapes=[dma(4), dma(4)],
        compiler_params=pltpu.CompilerParams(collective_id=2, has_side_effects=True),
    )(x_rim, y_rim)
    again = pl.pallas_call(
        functools.partial(second_kernel, grid_x, grid_y),
        out_shape=field,
        in_specs=[VMEM] * 10,
        out_specs=VMEM,
    )(first, kappa_sq, scaling, *rims, held, weights, cells)
    out = pl.pallas_call(
        finish_kernel,
        out_shape=field,
        in_specs=[VMEM] * 5,
        out_specs=VMEM,
    )(lines, again, gathered(again), prior, first)
    return out[None]


def solution(mesh):
    return jax.shard_map(
        shards,
        mesh=mesh,
        in_specs=(
            P("member", None, "gx", "gy"),
            P(),
            P(None, "gx", "gy"),
            P(None, "gx", "gy"),
            P("gx", None, None, None),
            P(None, ("gx", "gy")),
            P("member", ("gx", "gy")),
            P(("gx", "gy"), None),
            P(("gx", "gy")),
        ),
        out_specs=P("member", None, "gx", "gy"),
        check_vma=False,
    )
```

time: 176 us -> 101 us (0.57)
  blocking collectives: 100 us -> 0 us
  Pallas kernels: 11.1 us -> 99.1 us
  waiting for transfers between devices: 23.9 us -> 0 us
  between operations: 13.6 us -> 0.04 us
  starting transfers between devices: 12.2 us -> 0 us
  local copies, waits for them, and re-layouts: 6.54 us -> 1.53 us
  other arithmetic: 4.15 us -> 0 us
  matrix products: 2.5 us -> 0 us
    all_to_all x4 -> x0, blocking collectives: 100 us -> none  [the longest x2 49.3 us: precondition(): lax.all_to_all(field, 'gx', split_axis=0, concat_axis=1, tiled=True)]
    pallas_call x3 -> x9, Pallas kernels: 11.1 us -> 99.1 us  [the longest x1 40 us: shards(): pl.pallas_call(functools.partial(spread_kernel, members, grid_x, grid_y),...]
    all_to_all x1 -> x0, waiting for transfers between devices: 16.1 us -> none  [precondition(): lax.all_to_all(solved.reshape(pencil.shape), 'gx', split_axis=1, concat_a...]
    ppermute x4 -> x0, starting transfers between devices: 8.74 us -> none  [the longest x2 5.05 us: neighbours(): lax.ppermute(high_side, axis, forward)]
    reduce_scatter x1 -> x0, waiting for transfers between devices: 4.65 us -> none  [shards(): lax.psum_scatter(picked[:, None, None, None] * background, 'member', scat...]
    all_to_all x1 -> x0, starting transfers between devices: 3.47 us -> none  [precondition(): lax.all_to_all(solved.reshape(pencil.shape), 'gx', split_axis=1, concat_a...]
    ppermute x4 -> x0, waiting for transfers between devices: 3.22 us -> none  [the longest x2 3.22 us: neighbours(): lax.ppermute(low_side, axis, backward)]
    mul x4 -> x0, other arithmetic: 2.75 us -> none  [the longest x1 2.72 us: shards(): picked[:, None, None, None] * background]
  transfers between devices with their start and end apart: 6 -> 0, of which waited for: 3 -> 0; matrix products, arithmetic and copies ran while one was open for 2% -> 0% of each run, Pallas kernels for 2% -> 0%
where the time goes in v2:
time: 101 us
  Pallas kernels  99.1 us (98%)
  local copies, waits for them, and re-layouts  1.53 us (2%)
    pallas_call x1, Pallas kernels, shards(): pl.pallas_call(functools.partial(spread_kernel, members, grid_x, grid_y),...  40 us
    pallas_call x2, Pallas kernels, gathered(): pl.pallas_call(gather_kernel, out_shape=shape(4, depth, width_x, width_y)...  33.8 us
    pallas_call x1, Pallas kernels, shards(): pl.pallas_call(functools.partial(rim_kernel, grid_x, grid_y), out_shape=[...  6.14 us
    pallas_call x1, Pallas kernels, shards(): pl.pallas_call(functools.partial(first_kernel, slot_cap, members), out_sh...  4.65 us
    pallas_call x1, Pallas kernels, shards(): pl.pallas_call(functools.partial(second_kernel, grid_x, grid_y), out_shap...  4.43 us
    pallas_call x1, Pallas kernels, shards(): pl.pallas_call(finish_kernel, out_shape=field, in_specs=[VMEM] * 5, out_s...  3.71 us
    pallas_call x1, Pallas kernels, shards(): pl.pallas_call(solve_kernel, out_shape=(field, shape(2 * depth, width_y),...  3.57 us
    pallas_call x1, Pallas kernels, shards(): pl.pallas_call(functools.partial(place_kernel, slot_cap, grid_y), out_sha...  2.77 us

profile of v2, /device:TPU:1, one launch (start us, length us, event | category | flops | bytes accessed | tf_op | source)
XLA Modules:
  0.0 100.6 jit_solution(15860262826530940998)
XLA Ops:
  0.0 1.5 %copy.10.owner_col = s32[512,1]{1,0:T(8,128)} copy(s32[512,1]{0,1:T(1,128)} %param.16) | data formatting | bytes 4096 | tf_op args[7]
  1.5 2.8 %shard_map.91 = f32[128,2,128]{2,1,0:T(2,128)} custom-call(s32[512,1]{1,0:T(8,128)} %copy.10.owner_col, s32[1,512]{1,0:T(1,128)} %bitcast.12, f32[16,512]{1,0:T(8,128)} %panels.1, f32[1,512]{1,0:T(1,128)} %values.1, s32[1,512]{1,0:T(1,128)} %bitcast.13), custom_call_target="tpu_custom_call" | custom-call | tf_op jit(solution)/shard_map/pallas_call | solution.py:365
  4.3 40.0 %shard_map.92 = (f32[3,16,64,128]{3,2,1,0:T(8,128)}, f32[16,64,256]{2,1,0:T(8,128)}, f32[16,8,2,128]{3,2,1,0:T(2,128)}) custom-call(f32[16,64,128]{2,1,0:T(8,128)} %bitcast.7, f32[4,256,256]{2,1,0:T(8,128)} %bitcast.9, f32[8,16,2,128]{3,2,1,0:T(2,128)} %bitcast.10), custom_call_target="tpu_custom_call" | custom-call | tf_op jit(solution)/shard_map/pallas_call | solution.py:372
  44.3 4.6 %shard_map.93 = (f32[16,64,128]{2,1,0:T(8,128)}, f32[16,64,128]{2,1,0:T(8,128)}, f32[16,1024]{1,0:T(8,128)}, f32[1,1024]{1,0:T(1,128)}, s32[1,1024]{1,0:T(1,128)}) custom-call(f32[4,4]{1,0:T(4,128)} %mixing.1, f32[16,64,128]{2,1,0:T(8,128)} %bitcast.8, f32[3,16,64,128]{3,2,1,0:T(8,128)} %get-tuple-element.21.others, f32[128,2,128]{2,1,0:T(2,128)} %bitcast.11), custom_call_target="tpu_custom_call" | custom-call | tf_op jit(solution)/shard_map/pallas_call | solution.py:391
  48.9 16.8 %shard_map.94.whole = f32[4,16,64,128]{3,2,1,0:T(8,128)} custom-call(f32[16,64,128]{2,1,0:T(8,128)} %get-tuple-element.23.field), custom_call_target="tpu_custom_call" | custom-call | tf_op jit(solution)/shard_map/pallas_call | solution.py:405
  65.7 3.6 %shard_map.95 = (f32[16,64,128]{2,1,0:T(8,128)}, f32[32,128]{1,0:T(8,128)}, f32[64,128]{1,0:T(8,128)}) custom-call(f32[16,64,256]{2,1,0:T(8,128)} %get-tuple-element.20.lines, f32[16,64,128]{2,1,0:T(8,128)} %get-tuple-element.23.field, f32[4,16,64,128]{3,2,1,0:T(8,128)} %shard_map.94.whole, f32[16,64,128]{2,1,0:T(8,128)} %scaling.3), custom_call_target="tpu_custom_call" | custom-call | tf_op jit(solution)/shard_map/pallas_call | solution.py:414
  69.3 6.1 %shard_map.96 = (f32[32,128]{1,0:T(8,128)}, f32[32,128]{1,0:T(8,128)}, f32[64,128]{1,0:T(8,128)}, f32[64,128]{1,0:T(8,128)}) custom-call(f32[32,128]{1,0:T(8,128)} %get-tuple-element.25.x_rim, f32[64,128]{1,0:T(8,128)} %get-tuple-element.26.y_rim), custom_call_target="tpu_custom_call" | custom-call | tf_op jit(solution)/shard_map/pallas_call | solution.py:420
  75.4 4.4 %shard_map.97.field = f32[16,64,128]{2,1,0:T(8,128)} custom-call(f32[16,64,128]{2,1,0:T(8,128)} %get-tuple-element.24.first, f32[16,64,128]{2,1,0:T(8,128)} %kappa.1, f32[16,64,128]{2,1,0:T(8,128)} %scaling.3, f32[32,128]{1,0:T(8,128)} %get-tuple-element.27.x_low, f32[32,128]{1,0:T(8,128)} %get-tuple-element.28.x_high, f32[64,128]{1,0:T(8,128)} %get-tuple-element.29.y_low, ...), custom_call_target="tpu_custom_call" | custom-call | tf_op jit(solution)/shard_map/pallas_call | solution.py:428
  79.9 17.1 %shard_map.98.whole = f32[4,16,64,128]{3,2,1,0:T(8,128)} custom-call(f32[16,64,128]{2,1,0:T(8,128)} %shard_map.97.field), custom_call_target="tpu_custom_call" | custom-call | tf_op jit(solution)/shard_map/pallas_call | solution.py:405
  96.9 3.7 %shard_map.99 = f32[16,64,128]{2,1,0:T(8,128)} custom-call(f32[16,64,256]{2,1,0:T(8,128)} %get-tuple-element.20.lines, f32[16,64,128]{2,1,0:T(8,128)} %shard_map.97.field, f32[4,16,64,128]{3,2,1,0:T(8,128)} %shard_map.98.whole, f32[16,64,128]{2,1,0:T(8,128)} %get-tuple-element.34.prior, f32[16,64,128]{2,1,0:T(8,128)} %get-tuple-element.24.first), custom_call_target="tpu_custom_call" | custom-call | tf_op jit(solution)/shard_map/pallas_call | solution.py:434

commit v3 on v2

--- a/solution.py
+++ b/solution.py
@@ -21,23 +21,21 @@
     return high, (value - high.astype(F32)).astype(BF16)
 
 
-def place_kernel(slot_cap, grid_y, owner_col, owner_row, panels, values, spots, sent):
-    count = owner_col.shape[0]
+def place_kernel(slot_cap, grid_y, owner_row, panels, values, spots, sent):
+    count = owner_row.shape[1]
     tiles = sent.shape[0]
     depth = panels.shape[0]
     grid_x = tiles // grid_y
-    column = (owner_col[...] % grid_y) * grid_x + owner_col[...] // grid_y
     across = (owner_row[...] % grid_y) * grid_x + owner_row[...] // grid_y
-    own = lax.broadcasted_iota(jnp.int32, (count, tiles), 1) == column
-    hits = jnp.where(own, 1.0, 0.0).astype(F32)
+    mine = lax.broadcasted_iota(jnp.int32, (tiles, count), 0) == across
+    hits_t = jnp.where(mine, 1.0, 0.0).astype(F32)
+    hits = hits_t.T
     later = lax.broadcasted_iota(jnp.int32, (count, count), 0)
     sooner = lax.broadcasted_iota(jnp.int32, (count, count), 1)
     earlier = jnp.where(later > sooner, 1.0, 0.0).astype(BF16)
     before = jnp.dot(earlier, hits.astype(BF16), preferred_element_type=F32)
     rank = jnp.sum(before * hits, axis=1, keepdims=True).astype(jnp.int32)
-    mine = lax.broadcasted_iota(jnp.int32, (tiles, count), 0) == across
-    hits_t = jnp.where(mine, 1.0, 0.0).astype(BF16)
-    hits_t = jnp.concatenate([hits_t, hits_t], axis=1)
+    hits_t = jnp.concatenate([hits_t, hits_t], axis=1).astype(BF16)
     lane = lax.broadcasted_iota(jnp.int32, (count, slot_cap * depth), 1)
     stacked = jnp.concatenate([panels[...]] * slot_cap, axis=0).T
     body = jnp.where(lane // depth == rank, stacked, 0.0)
@@ -201,55 +199,136 @@
         copy.wait_send()
 
 
-def gather_kernel(field, whole, far_send, far_recv, near_send, near_recv, pass_send, pass_recv):
-    g = lax.axis_index("gx")
+def steps_kernel(
+    grid_x, grid_y, resid, panels, weights, cells, lines_in, scaling_in, kappa_in, prior_in, out,
+    whole, again, first, lines, scaling, kappa, prior, x_rim, y_rim, x_low, x_high, y_low, y_high,
+    far_send, far_recv, near_send, near_recv, pass_send, pass_recv, rim_send, rim_recv, here,
+):
+    depth, width_x, width_y = resid.shape
+    g, h = lax.axis_index("gx"), lax.axis_index("gy")
     flip = 2 - 4 * ((g // 2) % 2)
-    near = {"gx": g + 1 - 2 * (g % 2)}
-    far = {"gx": g + flip}
-    greet([near, far])
-    chunks = far_send.shape[0]
-    size = field.shape[0] // chunks
+    turn = 1 - 2 * (g % 2)
     place, other = g % 4, (g + flip) % 4
+    near, far = {"gx": g + turn}, {"gx": g + flip}
+    side = {"gx": (g - turn + grid_x) % grid_x}
+    up_y, down_y = {"gy": (h + 1) % grid_y}, {"gy": (h + grid_y - 1) % grid_y}
+    fetched = [
+        pltpu.make_async_copy(source, target, here.at[k])
+        for k, (source, target) in enumerate(
+            [(lines_in, lines), (scaling_in, scaling), (kappa_in, kappa), (prior_in, prior)]
+        )
+    ]
+    greet([near, far, side, up_y, down_y])
+
+    size = 4
+    chunks = depth // size
     spans = [pl.ds(c * size, size) for c in range(chunks)]
-    outs, ins, passed = [], [], []
-    for c, span in enumerate(spans):
-        outs.append(remote(field.at[span], whole.at[place, span], far_send.at[c], far_recv.at[c], far))
-        outs[-1].start()
-    for c, span in enumerate(spans):
-        ins.append(remote(field.at[span], whole.at[place, span], near_send.at[c], near_recv.at[c], near))
-        ins[-1].start()
-    for c, span in enumerate(spans):
-        outs[c].wait_recv()
-        passed.append(
-            remote(whole.at[other, span], whole.at[other, span], pass_send.at[c], pass_recv.at[c], near)
-        )
-        passed[-1].start()
-    for copy in ins + passed:
+
+    def start_chunk(source, target, c, k):
+        to_far = remote(source, target.at[place, spans[c]], far_send.at[k], far_recv.at[k], far)
+        to_near = remote(source, target.at[place, spans[c]], near_send.at[k], near_recv.at[k], near)
+        to_far.start()
+        to_near.start()
+        return to_far, to_near
+
+    def solve(target, sent, base, use):
+        passed = []
+
+        def finish(c):
+            sent[c][1].wait_recv()
+            passed[c].wait_recv()
+            for z in range(c * size, c * size + size):
+                rows = jnp.concatenate([target[p, z] for p in range(4)], axis=0)
+                left = jnp.concatenate(halves(lines[z]), axis=0)
+                both = jnp.concatenate(halves(rows), axis=1)
+                full = jnp.dot(left, both, preferred_element_type=F32)
+                use(z, full[:width_x, :width_y] + (full[width_x:, :width_y] + full[:width_x, width_y:]))
+
+        for c in range(chunks):
+            sent[c][0].wait_recv()
+            came = target.at[other, spans[c]]
+            passed.append(remote(came, came, pass_send.at[base + c], pass_recv.at[base + c], near))
+            passed[c].start()
+            if c > 0:
+                finish(c - 1)
+        finish(chunks - 1)
+        for c in range(chunks):
+            sent[c][0].wait_send()
+            sent[c][1].wait_send()
+            passed[c].wait_send()
+
+    sent = [start_chunk(resid.at[spans[c]], whole, c, c) for c in range(chunks)]
+    mine = pltpu.make_async_copy(resid, whole.at[place], here.at[4])
+    mine.start()
+    for copy in fetched:
+        copy.start()
+    at_x, at_y = masks(cells[...], width_x, width_y)
+    lane = lax.broadcasted_iota(jnp.int32, (width_x, width_y), 1)
+    row = lax.broadcasted_iota(jnp.int32, (width_x, width_y), 0)
+    mine.wait()
+    for copy in fetched:
         copy.wait()
-    for copy in outs:
-        copy.wait_send()
-
-
-def rim_kernel(grid_x, grid_y, x_rim, y_rim, x_low, x_high, y_low, y_high, sends, receives):
-    g, h = lax.axis_index("gx"), lax.axis_index("gy")
-    up_x, down_x = {"gx": (g + 1) % grid_x}, {"gx": (g + grid_x - 1) % grid_x}
-    up_y, down_y = {"gy": (h + 1) % grid_y}, {"gy": (h + grid_y - 1) % grid_y}
-    greet([up_x, down_x, up_y, down_y])
-    copies = [
-        remote(source, target, sends.at[k], receives.at[k], device)
+
+    rims = [jnp.zeros((width_x, width_y), F32)]
+
+    def use_first(z, level):
+        first[z] = level
+        scaled = scaling[z] * level
+        x_rim[z : z + 1] = scaled[:1]
+        x_rim[depth + z : depth + z + 1] = scaled[width_x - 1 :]
+        low = jnp.where(lane == z, scaled[:, :1], rims[0])
+        rims[0] = jnp.where(lane == depth + z, scaled[:, width_y - 1 :], low)
+
+    solve(whole, sent, 0, use_first)
+    y_rim[...] = rims[0]
+    edges = [
+        remote(source, target, rim_send.at[k], rim_recv.at[k], device)
         for k, (source, target, device) in enumerate(
             [
-                (x_rim, x_low, up_x),
-                (x_rim, x_high, down_x),
+                (x_rim, x_low, {"gx": (g + 1) % grid_x}),
+                (x_rim, x_high, {"gx": (g + grid_x - 1) % grid_x}),
                 (y_rim, y_low, up_y),
                 (y_rim, y_high, down_y),
             ]
         )
     ]
-    for copy in copies:
+    for copy in edges:
         copy.start()
-    for copy in copies:
+    left = weights[...] - project(first, panels, at_x, at_y)
+    for copy in edges:
         copy.wait()
+    low_x = jnp.where(g > 0, x_low[...], 0.0)
+    high_x = jnp.where(g < grid_x - 1, x_high[...], 0.0)
+    low_y = jnp.where(h > 0, y_low[...], 0.0)
+    high_y = jnp.where(h < grid_y - 1, y_high[...], 0.0)
+    sent = []
+    for c in range(chunks):
+        summed = scattered(left, panels, at_x, at_y, c * size)
+        for k in range(c * size, c * size + size):
+            here_u = scaling[k] * first[k]
+            beside = jnp.where(row == 0, low_x[depth + k : depth + k + 1], pltpu.roll(here_u, 1, 0))
+            beside = beside + jnp.where(
+                row == width_x - 1, high_x[k : k + 1], pltpu.roll(here_u, width_x - 1, 0)
+            )
+            beside = beside + jnp.where(
+                lane == 0, low_y[:, depth + k : depth + k + 1], pltpu.roll(here_u, 1, 1)
+            )
+            beside = beside + jnp.where(
+                lane == width_y - 1, high_y[:, k : k + 1], pltpu.roll(here_u, width_y - 1, 1)
+            )
+            if k > 0:
+                beside = beside + scaling[k - 1] * first[k - 1]
+            if k < depth - 1:
+                beside = beside + scaling[k + 1] * first[k + 1]
+            again[place, k] = summed[k - c * size] - (
+                kappa[k] * first[k] + scaling[k] * (6.0 * here_u - beside)
+            )
+        sent.append(start_chunk(again.at[place, spans[c]], again, c, chunks + c))
+
+    def use_second(z, level):
+        out[z] = prior[z] + (first[z] + level)
+
+    solve(again, sent, chunks, use_second)
 
 
 def first_kernel(slot_cap, members, mixing, background, others, got, prior, resid, panels, weights, cells):
@@ -274,74 +353,6 @@
     weights[...] = left
     for z in range(0, depth, 4):
         resid[z : z + 4] = scattered(left, panels, at_x, at_y, z)
-
-
-def solved_level(lines, field, whole, z):
-    place = lax.axis_index("gx") % 4
-    rows = jnp.concatenate(
-        [jnp.where(place == p, field[z], whole[p, z]) for p in range(4)], axis=0
-    )
-    left = jnp.concatenate(halves(lines[z]), axis=0)
-    out = jnp.dot(left, jnp.concatenate(halves(rows), axis=1), preferred_element_type=F32)
-    width_x, width_y = field.shape[1:]
-    return out[:width_x, :width_y] + (out[width_x:, :width_y] + out[:width_x, width_y:])
-
-
-def solve_kernel(lines, field, whole, scaling, first, x_rim, y_rim):
-    depth, width_x, width_y = field.shape
-    lane = lax.broadcasted_iota(jnp.int32, (width_x, width_y), 1)
-    rims = jnp.zeros((width_x, width_y), F32)
-    for z in range(depth):
-        level = solved_level(lines, field, whole, z)
-        first[z] = level
-        scaled = scaling[z] * level
-        x_rim[z : z + 1] = scaled[:1]
-        x_rim[depth + z : depth + z + 1] = scaled[width_x - 1 :]
-        rims = jnp.where(lane == z, scaled[:, :1], rims)
-        rims = jnp.where(lane == depth + z, scaled[:, width_y - 1 :], rims)
-    y_rim[...] = rims
-
-
-def finish_kernel(lines, field, whole, prior, first, out):
-    for z in range(field.shape[0]):
-        out[z] = prior[z] + (first[z] + solved_level(lines, field, whole, z))
-
-
-def second_kernel(
-    grid_x, grid_y, first, kappa, scaling, x_low, x_high, y_low, y_high, panels, weights, cells, resid
-):
-    depth, width_x, width_y = first.shape
-    g, h = lax.axis_index("gx"), lax.axis_index("gy")
-    at_x, at_y = masks(cells[...], width_x, width_y)
-    left = weights[...] - project(first, panels, at_x, at_y)
-    column = lax.broadcasted_iota(jnp.int32, (width_x, width_y), 1)
-    row = lax.broadcasted_iota(jnp.int32, (width_x, width_y), 0)
-    low_x = jnp.where(g > 0, x_low[...], 0.0)
-    high_x = jnp.where(g < grid_x - 1, x_high[...], 0.0)
-    low_y = jnp.where(h > 0, y_low[...], 0.0)
-    high_y = jnp.where(h < grid_y - 1, y_high[...], 0.0)
-    levels = [scaling[z] * first[z] for z in range(depth)]
-    for z in range(0, depth, 4):
-        summed = scattered(left, panels, at_x, at_y, z)
-        for k in range(z, z + 4):
-            here = levels[k]
-            beside = jnp.where(row == 0, low_x[depth + k : depth + k + 1], pltpu.roll(here, 1, 0))
-            beside = beside + jnp.where(
-                row == width_x - 1, high_x[k : k + 1], pltpu.roll(here, width_x - 1, 0)
-            )
-            beside = beside + jnp.where(
-                column == 0, low_y[:, depth + k : depth + k + 1], pltpu.roll(here, 1, 1)
-            )
-            beside = beside + jnp.where(
-                column == width_y - 1, high_y[:, k : k + 1], pltpu.roll(here, width_y - 1, 1)
-            )
-            if k > 0:
-                beside = beside + levels[k - 1]
-            if k < depth - 1:
-                beside = beside + levels[k + 1]
-            resid[k] = summed[k - z] - (
-                kappa[k] * first[k] + scaling[k] * (6.0 * here - beside)
-            )
 
 
 def shape(*dims, dtype=F32):
@@ -365,9 +376,9 @@
     sent = pl.pallas_call(
         functools.partial(place_kernel, slot_cap, grid_y),
         out_shape=shape(tiles, 2, slot_cap * depth),
-        in_specs=[VMEM] * 5,
+        in_specs=[VMEM] * 4,
         out_specs=VMEM,
-    )(targets, targets.reshape(1, count), panels, values, spots.reshape(1, count))
+    )(targets.reshape(1, count), panels, values, spots.reshape(1, count))
     pair = (2, slot_cap * depth)
     others, lines, got = pl.pallas_call(
         functools.partial(spread_kernel, members, grid_x, grid_y),
@@ -401,42 +412,22 @@
         out_specs=[VMEM] * 5,
     )(mixing, background, others, got.reshape(tiles, *pair))
 
-    def gathered(piece):
-        return pl.pallas_call(
-            gather_kernel,
-            out_shape=shape(4, depth, width_x, width_y),
-            in_specs=[ANY],
-            out_specs=ANY,
-            scratch_shapes=[dma(4)] * 6,
-            compiler_params=pltpu.CompilerParams(collective_id=1, has_side_effects=True),
-        )(piece)
-
-    first, x_rim, y_rim = pl.pallas_call(
-        solve_kernel,
-        out_shape=(field, shape(2 * depth, width_y), shape(width_x, width_y)),
-        in_specs=[VMEM] * 4,
-        out_specs=[VMEM] * 3,
-    )(lines, resid, gathered(resid), scaling)
-    rims = pl.pallas_call(
-        functools.partial(rim_kernel, grid_x, grid_y),
-        out_shape=[shape(2 * depth, width_y)] * 2 + [shape(width_x, width_y)] * 2,
-        in_specs=[VMEM] * 2,
-        out_specs=[VMEM] * 4,
-        scratch_shapes=[dma(4), dma(4)],
-        compiler_params=pltpu.CompilerParams(collective_id=2, has_side_effects=True),
-    )(x_rim, y_rim)
-    again = pl.pallas_call(
-        functools.partial(second_kernel, grid_x, grid_y),
+    block = pltpu.VMEM((depth, width_x, width_y), F32)
+    gathered = pltpu.VMEM((4, depth, width_x, width_y), F32)
+    x_edge = pltpu.VMEM((2 * depth, width_y), F32)
+    y_edge = pltpu.VMEM((width_x, width_y), F32)
+    out = pl.pallas_call(
+        functools.partial(steps_kernel, grid_x, grid_y),
         out_shape=field,
-        in_specs=[VMEM] * 10,
+        in_specs=[VMEM] * 4 + [ANY] * 4,
         out_specs=VMEM,
-    )(first, kappa_sq, scaling, *rims, held, weights, cells)
-    out = pl.pallas_call(
-        finish_kernel,
-        out_shape=field,
-        in_specs=[VMEM] * 5,
-        out_specs=VMEM,
-    )(lines, again, gathered(again), prior, first)
+        scratch_shapes=[
+            gathered, gathered, block, pltpu.VMEM((depth, width_x, line), F32), block, block, block,
+            x_edge, y_edge, x_edge, x_edge, y_edge, y_edge,
+            dma(8), dma(8), dma(8), dma(8), dma(8), dma(8), dma(4), dma(4), dma(5),
+        ],
+        compiler_params=pltpu.CompilerParams(collective_id=1, has_side_effects=True),
+    )(resid, held, weights, cells, lines, scaling, kappa_sq, prior)
     return out[None]
 
 

time: 101 us -> 87.3 us (0.86)
  Pallas kernels: 99.1 us -> 85 us
    pallas_call x6 -> x1, Pallas kernels: 51.7 us -> 38 us  [shards(): pl.pallas_call(functools.partial(steps_kernel, grid_x, grid_y), out_shape...]
where the time goes in v3:
time: 87.3 us; the launch traced here: 86.9 us
  Pallas kernels  85 us (97%)
  local copies, waits for them, and re-layouts  1.89 us (2%)
    pallas_call x1, Pallas kernels, shards(): pl.pallas_call(functools.partial(spread_kernel, members, grid_x, grid_y),...  40 us
    pallas_call x1, Pallas kernels, shards(): pl.pallas_call(functools.partial(steps_kernel, grid_x, grid_y), out_shape...  38 us
    pallas_call x1, Pallas kernels, shards(): pl.pallas_call(functools.partial(first_kernel, slot_cap, members), out_sh...  4.67 us
    pallas_call x1, Pallas kernels, shards(): pl.pallas_call(functools.partial(place_kernel, slot_cap, grid_y), out_sha...  2.43 us
    unnamed x1, local copies, waits for them, and re-layouts  1.89 us

profile of v3, /device:TPU:1, one launch (start us, length us, event | category | flops | bytes accessed | tf_op | source)
XLA Modules:
  0.0 86.9 jit_solution(3025398106453142922)
XLA Ops:
  0.0 2.4 %shard_map.91 = f32[128,2,128]{2,1,0:T(2,128)} custom-call(s32[1,512]{1,0:T(1,128)} %bitcast.13, f32[16,512]{1,0:T(8,128)} %panels.1, f32[1,512]{1,0:T(1,128)} %values.1, s32[1,512]{1,0:T(1,128)} %bitcast.14), custom_call_target="tpu_custom_call" | custom-call | tf_op jit(solution)/shard_map/pallas_call | solution.py:376
  2.4 40.0 %shard_map.92 = (f32[3,16,64,128]{3,2,1,0:T(8,128)}, f32[16,64,256]{2,1,0:T(8,128)}, f32[16,8,2,128]{3,2,1,0:T(2,128)}) custom-call(f32[16,64,128]{2,1,0:T(8,128)} %bitcast.7, f32[4,256,256]{2,1,0:T(8,128)} %bitcast.10, f32[8,16,2,128]{3,2,1,0:T(2,128)} %bitcast.11), custom_call_target="tpu_custom_call" | custom-call | tf_op jit(solution)/shard_map/pallas_call | solution.py:383
  42.4 4.7 %shard_map.93 = (f32[16,64,128]{2,1,0:T(8,128)}, f32[16,64,128]{2,1,0:T(8,128)}, f32[16,1024]{1,0:T(8,128)}, f32[1,1024]{1,0:T(1,128)}, s32[1,1024]{1,0:T(1,128)}) custom-call(f32[4,4]{1,0:T(4,128)} %mixing.1, f32[16,64,128]{2,1,0:T(8,128)} %bitcast.8, f32[3,16,64,128]{3,2,1,0:T(8,128)} %get-tuple-element.13.others, f32[128,2,128]{2,1,0:T(2,128)} %bitcast.12), custom_call_target="tpu_custom_call" | custom-call | tf_op jit(solution)/shard_map/pallas_call | solution.py:402
  47.1 38.0 %shard_map.94 = f32[16,64,128]{2,1,0:T(8,128)} custom-call(f32[16,64,128]{2,1,0:T(8,128)} %get-tuple-element.15.resid, f32[16,1024]{1,0:T(8,128)} %get-tuple-element.16.panels, f32[1,1024]{1,0:T(1,128)} %get-tuple-element.17.weights, s32[1,1024]{1,0:T(1,128)} %get-tuple-element.18.cells, f32[16,64,256]{2,1,0:T(8,128)} %get-tuple-element.19.lines_in, ...), custom_call_target="tpu_custom_call" | custom-call | tf_op jit(solution)/shard_map/pallas_call | solution.py:419
  85.0 1.9 %copy.11 = f32[1,16,64,128]{3,2,1,0:T(8,128)} copy(f32[1,16,64,128]{3,2,1,0:T(8,128)} %bitcast.9) | data formatting | bytes 1048576

commit v4 on v3

--- a/solution.py
+++ b/solution.py
@@ -107,8 +107,8 @@
     )
 
 
-def spread_kernel(
-    members, grid_x, grid_y, background, line, sent, others, lines, got, mid,
+def spread(
+    members, grid_x, grid_y, fill, background, line, sent, others, lines, got, mid,
     own_send, own_recv, relay_send, relay_recv, line_send, line_recv, pass_send, pass_recv,
     y_send, y_recv, x_send, x_recv, here,
 ):
@@ -127,14 +127,6 @@
     quads = line.shape[1] // wide
     start = pl.multiple_of((h % 2) * part, part)
 
-    stations = [
-        remote(sent.at[(h + d) % grid_y], mid.at[h], y_send.at[d - 1], y_recv.at[d - 1], along_y[d - 1])
-        for d in range(1, grid_y)
-    ]
-    for copy in stations:
-        copy.start()
-    mine = pltpu.make_async_copy(sent.at[h], mid.at[h], here.at[0])
-    mine.start()
     own = [
         remote(background.at[piece], others.at[slot, piece], own_send.at[k], own_recv.at[k], device)
         for k, (piece, slot, device) in enumerate(
@@ -161,16 +153,25 @@
     level = pltpu.make_async_copy(line.at[g // quads, mine_rows], lines.at[g], here.at[1])
     level.start()
 
+    fill()
+    stations = [
+        remote(sent.at[pl.ds((h + d) % grid_y * grid_x, grid_x)], mid.at[h], y_send.at[d - 1], y_recv.at[d - 1], along_y[d - 1])
+        for d in range(1, grid_y)
+    ]
+    for copy in stations:
+        copy.start()
+    mine = pltpu.make_async_copy(sent.at[pl.ds(h * grid_x, grid_x)], mid.at[h], here.at[0])
+    mine.start()
     mine.wait()
     for copy in stations:
         copy.wait_recv()
     second = [
-        remote(mid.at[:, (g + d) % grid_x], got.at[g], x_send.at[d - 1], x_recv.at[d - 1], along_x[d - 1])
+        remote(mid.at[:, (g + d) % grid_x], got.at[pl.ds(g * grid_y, grid_y)], x_send.at[d - 1], x_recv.at[d - 1], along_x[d - 1])
         for d in range(1, grid_x)
     ]
     for copy in second:
         copy.start()
-    last = pltpu.make_async_copy(mid.at[:, g], got.at[g], here.at[2])
+    last = pltpu.make_async_copy(mid.at[:, g], got.at[pl.ds(g * grid_y, grid_y)], here.at[2])
     last.start()
 
     own[0].wait_recv()
@@ -199,26 +200,60 @@
         copy.wait_send()
 
 
+def unpack(slot_cap, got, panels, weights, cells):
+    depth, tiles = panels.shape[0], got.shape[0]
+    body = got[:, 0, :].T
+    extra = got[:, 1, :].T
+    for k in range(slot_cap):
+        lanes = pl.ds(k * tiles, tiles)
+        panels[:, lanes] = body[k * depth : (k + 1) * depth]
+        weights[:, lanes] = extra[k : k + 1]
+        cells[:, lanes] = extra[slot_cap + k : slot_cap + k + 1].astype(jnp.int32)
+
+
 def steps_kernel(
-    grid_x, grid_y, resid, panels, weights, cells, lines_in, scaling_in, kappa_in, prior_in, out,
-    whole, again, first, lines, scaling, kappa, prior, x_rim, y_rim, x_low, x_high, y_low, y_high,
+    members, grid_x, grid_y, slot_cap,
+    mixing, owner_row, panels_in, values, spots, background, line, scaling_in, kappa_in, prior, out,
+    sent_slots, mid, got, others, mine_field, panels, weights, cells,
+    whole, again, first, lines, scaling, kappa, x_rim, y_rim, x_low, x_high, y_low, y_high,
+    own_send, own_recv, relay_send, relay_recv, line_send, line_recv, hand_send, hand_recv,
+    y_send, y_recv, x_send, x_recv, there,
     far_send, far_recv, near_send, near_recv, pass_send, pass_recv, rim_send, rim_recv, here,
 ):
-    depth, width_x, width_y = resid.shape
+    depth, width_x, width_y = out.shape
+    m = lax.axis_index("member")
     g, h = lax.axis_index("gx"), lax.axis_index("gy")
     flip = 2 - 4 * ((g // 2) % 2)
     turn = 1 - 2 * (g % 2)
     place, other = g % 4, (g + flip) % 4
     near, far = {"gx": g + turn}, {"gx": g + flip}
-    side = {"gx": (g - turn + grid_x) % grid_x}
     up_y, down_y = {"gy": (h + 1) % grid_y}, {"gy": (h + grid_y - 1) % grid_y}
     fetched = [
         pltpu.make_async_copy(source, target, here.at[k])
         for k, (source, target) in enumerate(
-            [(lines_in, lines), (scaling_in, scaling), (kappa_in, kappa), (prior_in, prior)]
+            [(background, mine_field), (scaling_in, scaling), (kappa_in, kappa)]
         )
     ]
-    greet([near, far, side, up_y, down_y])
+    for copy in fetched:
+        copy.start()
+
+    def fill():
+        place_kernel(slot_cap, grid_y, owner_row, panels_in, values, spots, sent_slots)
+
+    spread(
+        members, grid_x, grid_y, fill, background, line, sent_slots, others, lines, got, mid,
+        own_send, own_recv, relay_send, relay_recv, line_send, line_recv, hand_send, hand_recv,
+        y_send, y_recv, x_send, x_recv, there,
+    )
+    for copy in fetched:
+        copy.wait()
+    prior[...] = (
+        mixing[m, m] * mine_field[...]
+        + mixing[m, (m + members - 1) % members] * others[0]
+        + mixing[m, (m + 1) % members] * others[1]
+        + mixing[m, (m + 2) % members] * others[2]
+    )
+    unpack(slot_cap, got, panels, weights, cells)
 
     size = 4
     chunks = depth // size
@@ -257,17 +292,14 @@
             sent[c][1].wait_send()
             passed[c].wait_send()
 
-    sent = [start_chunk(resid.at[spans[c]], whole, c, c) for c in range(chunks)]
-    mine = pltpu.make_async_copy(resid, whole.at[place], here.at[4])
-    mine.start()
-    for copy in fetched:
-        copy.start()
     at_x, at_y = masks(cells[...], width_x, width_y)
     lane = lax.broadcasted_iota(jnp.int32, (width_x, width_y), 1)
     row = lax.broadcasted_iota(jnp.int32, (width_x, width_y), 0)
-    mine.wait()
-    for copy in fetched:
-        copy.wait()
+    weights[...] = weights[...] - project(prior, panels, at_x, at_y)
+    sent = []
+    for c in range(chunks):
+        whole[place, spans[c]] = scattered(weights[...], panels, at_x, at_y, c * size)
+        sent.append(start_chunk(whole.at[place, spans[c]], whole, c, c))
 
     rims = [jnp.zeros((width_x, width_y), F32)]
 
@@ -326,33 +358,9 @@
         sent.append(start_chunk(again.at[place, spans[c]], again, c, chunks + c))
 
     def use_second(z, level):
-        out[z] = prior[z] + (first[z] + level)
+        out[z] = first[z] + level
 
     solve(again, sent, chunks, use_second)
-
-
-def first_kernel(slot_cap, members, mixing, background, others, got, prior, resid, panels, weights, cells):
-    depth, width_x, width_y = background.shape
-    tiles = got.shape[0]
-    m = lax.axis_index("member")
-    prior[...] = (
-        mixing[m, m] * background[...]
-        + mixing[m, (m + members - 1) % members] * others[0]
-        + mixing[m, (m + 1) % members] * others[1]
-        + mixing[m, (m + 2) % members] * others[2]
-    )
-    body = got[:, 0, :].T
-    extra = got[:, 1, :].T
-    for k in range(slot_cap):
-        lanes = pl.ds(k * tiles, tiles)
-        panels[:, lanes] = body[k * depth : (k + 1) * depth]
-        weights[:, lanes] = extra[k : k + 1]
-        cells[:, lanes] = extra[slot_cap + k : slot_cap + k + 1].astype(jnp.int32)
-    at_x, at_y = masks(cells[...], width_x, width_y)
-    left = weights[...] - project(prior, panels, at_x, at_y)
-    weights[...] = left
-    for z in range(0, depth, 4):
-        resid[z : z + 4] = scattered(left, panels, at_x, at_y, z)
 
 
 def shape(*dims, dtype=F32):
@@ -373,62 +381,39 @@
     field = shape(depth, width_x, width_y)
     line = line_inverse.shape[2]
     background, line_inverse = background[0], line_inverse[0]
-    sent = pl.pallas_call(
-        functools.partial(place_kernel, slot_cap, grid_y),
-        out_shape=shape(tiles, 2, slot_cap * depth),
-        in_specs=[VMEM] * 4,
-        out_specs=VMEM,
-    )(targets.reshape(1, count), panels, values, spots.reshape(1, count))
-    pair = (2, slot_cap * depth)
-    others, lines, got = pl.pallas_call(
-        functools.partial(spread_kernel, members, grid_x, grid_y),
-        out_shape=(
-            shape(members - 1, depth, width_x, width_y),
-            shape(depth, width_x, line),
-            shape(grid_x, grid_y, *pair),
-        ),
-        in_specs=[ANY, ANY, VMEM],
-        out_specs=(ANY, ANY, VMEM),
-        scratch_shapes=[
-            pltpu.VMEM((grid_y, grid_x, *pair), F32),
-            dma(4), dma(4), dma(2), dma(2),
-            dma(grid_x - 1), dma(grid_x - 1), dma(grid_x - 1), dma(grid_x - 1),
-            dma(grid_y - 1), dma(grid_y - 1), dma(grid_x - 1), dma(grid_x - 1),
-            dma(3),
-        ],
-        compiler_params=pltpu.CompilerParams(collective_id=0, has_side_effects=True),
-    )(background, line_inverse, sent.reshape(grid_y, grid_x, *pair))
     slots = tiles * slot_cap
-    prior, resid, held, weights, cells = pl.pallas_call(
-        functools.partial(first_kernel, slot_cap, members),
-        out_shape=(
-            field,
-            field,
-            shape(depth, slots),
-            shape(1, slots),
-            shape(1, slots, dtype=jnp.int32),
-        ),
-        in_specs=[pl.BlockSpec(memory_space=pltpu.SMEM)] + [VMEM] * 3,
-        out_specs=[VMEM] * 5,
-    )(mixing, background, others, got.reshape(tiles, *pair))
-
+    packet = pltpu.VMEM((tiles, 2, slot_cap * depth), F32)
     block = pltpu.VMEM((depth, width_x, width_y), F32)
     gathered = pltpu.VMEM((4, depth, width_x, width_y), F32)
     x_edge = pltpu.VMEM((2 * depth, width_y), F32)
     y_edge = pltpu.VMEM((width_x, width_y), F32)
-    out = pl.pallas_call(
-        functools.partial(steps_kernel, grid_x, grid_y),
-        out_shape=field,
-        in_specs=[VMEM] * 4 + [ANY] * 4,
-        out_specs=VMEM,
+    far_x, far_y = grid_x - 1, grid_y - 1
+    prior, second = pl.pallas_call(
+        functools.partial(steps_kernel, members, grid_x, grid_y, slot_cap),
+        out_shape=(field, field),
+        in_specs=[pl.BlockSpec(memory_space=pltpu.SMEM)] + [VMEM] * 4 + [ANY] * 4,
+        out_specs=(VMEM, VMEM),
         scratch_shapes=[
-            gathered, gathered, block, pltpu.VMEM((depth, width_x, line), F32), block, block, block,
+            packet,
+            pltpu.VMEM((grid_y, grid_x, 2, slot_cap * depth), F32),
+            packet,
+            pltpu.VMEM((members - 1, depth, width_x, width_y), F32),
+            block,
+            pltpu.VMEM((depth, slots), F32),
+            pltpu.VMEM((1, slots), F32),
+            pltpu.VMEM((1, slots), jnp.int32),
+            gathered, gathered, block, pltpu.VMEM((depth, width_x, line), F32), block, block,
             x_edge, y_edge, x_edge, x_edge, y_edge, y_edge,
-            dma(8), dma(8), dma(8), dma(8), dma(8), dma(8), dma(4), dma(4), dma(5),
+            dma(4), dma(4), dma(2), dma(2), dma(far_x), dma(far_x), dma(far_x), dma(far_x),
+            dma(far_y), dma(far_y), dma(far_x), dma(far_x), dma(3),
+            dma(8), dma(8), dma(8), dma(8), dma(8), dma(8), dma(4), dma(4), dma(3),
         ],
-        compiler_params=pltpu.CompilerParams(collective_id=1, has_side_effects=True),
-    )(resid, held, weights, cells, lines, scaling, kappa_sq, prior)
-    return out[None]
+        compiler_params=pltpu.CompilerParams(collective_id=0, has_side_effects=True),
+    )(
+        mixing, targets.reshape(1, count), panels, values, spots.reshape(1, count),
+        background, line_inverse, scaling, kappa_sq,
+    )
+    return (prior + second)[None]
 
 
 def solution(mesh):

time: 87.3 us -> 77.8 us (0.89)
  Pallas kernels: 85 us -> 75.6 us
  other arithmetic: 0 us -> 2.06 us
  local copies, waits for them, and re-layouts: 1.89 us -> 0 us
    pallas_call x4 -> x1, Pallas kernels: 85 us -> 75.6 us  [shards(): pl.pallas_call(functools.partial(steps_kernel, members, grid_x, grid_y, s...]
    broadcast_in_dim x0 -> x1, other arithmetic: none -> 2.06 us  [shards(): return (prior + second)[None]]
    unnamed x1 -> x0, local copies, waits for them, and re-layouts: 1.89 us -> none
where the time goes in v4:
time: 77.8 us; the launch traced here: 77.6 us
  Pallas kernels  75.6 us (97%)
  other arithmetic  2.06 us (3%)
    pallas_call x1, Pallas kernels, shards(): pl.pallas_call(functools.partial(steps_kernel, members, grid_x, grid_y, s...  75.6 us
    broadcast_in_dim x1, other arithmetic, shards(): return (prior + second)[None]  2.06 us

profile of v4, /device:TPU:1, one launch (start us, length us, event | category | flops | bytes accessed | tf_op | source)
XLA Modules:
  0.0 77.6 jit_solution(2319879372869121280)
XLA Ops:
  0.0 75.6 %shard_map.91 = (f32[16,64,128]{2,1,0:T(8,128)}, f32[16,64,128]{2,1,0:T(8,128)}) custom-call(f32[4,4]{1,0:T(4,128)} %mixing.1, s32[1,512]{1,0:T(1,128)} %bitcast.8, f32[16,512]{1,0:T(8,128)} %panels_in.1, f32[1,512]{1,0:T(1,128)} %values.1, s32[1,512]{1,0:T(1,128)} %bitcast.9, f32[16,64,128]{2,1,0:T(8,128)} %bitcast.7, f32[4,256,256]{2,1,0:T(8,128)} %bitcast.6, ...), custom_call_target="tpu_custom_call" | custom-call | tf_op jit(solution)/shard_map/pallas_call | solution.py:391
  75.6 2.1 %add_bitcast_fusion = f32[1,16,64,128]{3,2,1,0:T(8,128)} fusion(f32[16,64,128]{2,1,0:T(8,128)} %get-tuple-element.7, f32[16,64,128]{2,1,0:T(8,128)} %get-tuple-element.8), kind=kLoop, calls=%fused_computation | loop fusion | flops 131072 | bytes 1572864 | tf_op jit(solution)/shard_map/broadcast_in_dim | solution.py:416

commit v5 on v4

--- a/solution.py
+++ b/solution.py
@@ -59,19 +59,16 @@
     return at_x, jnp.where(at_y, 1.0, 0.0).astype(BF16)
 
 
-def project(field, panels, at_x, at_y):
+def project(field, panels, at_x, at_y, z):
     depth, width_x, width_y = field.shape
     count = at_y.shape[1]
     both = jnp.concatenate([at_y, at_y], axis=0)
-    total = jnp.zeros((1, count), F32)
-    for z in range(0, depth, 4):
-        rows = field[z : z + 4].reshape(4 * width_x, width_y)
-        seen = jnp.dot(
-            jnp.concatenate(halves(rows), axis=1), both, preferred_element_type=F32
-        ).reshape(4, width_x, count)
-        seen = jnp.sum(jnp.where(at_x[None], seen, 0.0), axis=1)
-        total = total + jnp.sum(seen * panels[z : z + 4], axis=0, keepdims=True)
-    return total
+    rows = field[z : z + 4].reshape(4 * width_x, width_y)
+    seen = jnp.dot(
+        jnp.concatenate(halves(rows), axis=1), both, preferred_element_type=F32
+    ).reshape(4, width_x, count)
+    seen = jnp.sum(jnp.where(at_x[None], seen, 0.0), axis=1)
+    return jnp.sum(seen * panels[z : z + 4], axis=0, keepdims=True)
 
 
 def scattered(weights, panels, at_x, at_y, z):
@@ -108,7 +105,7 @@
 
 
 def spread(
-    members, grid_x, grid_y, fill, background, line, sent, others, lines, got, mid,
+    members, grid_x, grid_y, fill, ready, use, background, line, sent, others, lines, got, mid,
     own_send, own_recv, relay_send, relay_recv, line_send, line_recv, pass_send, pass_recv,
     y_send, y_recv, x_send, x_recv, here,
 ):
@@ -120,18 +117,18 @@
     mate = {"gy": h + 1 - 2 * (h % 2)}
     greet([right, left] + along_x + along_y)
 
-    half = background.shape[0] // 2
-    low, high = pl.ds(0, half), pl.ds(half, half)
+    chunks = own_send.shape[0] // 2
+    size = background.shape[0] // chunks
+    spans = [pl.ds(c * size, size) for c in range(chunks)]
     wide = lines.shape[1]
     part = wide // 2
     quads = line.shape[1] // wide
     start = pl.multiple_of((h % 2) * part, part)
 
     own = [
-        remote(background.at[piece], others.at[slot, piece], own_send.at[k], own_recv.at[k], device)
-        for k, (piece, slot, device) in enumerate(
-            [(low, 0, right), (high, 1, left), (high, 0, right), (low, 1, left)]
-        )
+        remote(background.at[span], others.at[slot, span], own_send.at[2 * c + slot], own_recv.at[2 * c + slot], device)
+        for c, span in enumerate(spans)
+        for slot, device in ((0, right), (1, left))
     ]
     for copy in own:
         copy.start()
@@ -174,30 +171,41 @@
     last = pltpu.make_async_copy(mid.at[:, g], got.at[pl.ds(g * grid_y, grid_y)], here.at[2])
     last.start()
 
-    own[0].wait_recv()
-    relay = [
-        remote(others.at[0, low], others.at[2, low], relay_send.at[0], relay_recv.at[0], right),
-        remote(others.at[1, high], others.at[2, high], relay_send.at[1], relay_recv.at[1], left),
-    ]
-    relay[0].start()
-    own[1].wait_recv()
-    relay[1].start()
-
+    relay = []
+    rows = background.shape[1] // 2
+    for c, span in enumerate(spans):
+        for slot, device in ((0, right), (1, left)):
+            k = 2 * c + slot
+            share = pl.ds(slot * rows, rows)
+            own[k].wait_recv()
+            relay.append(
+                remote(
+                    others.at[slot, span, share],
+                    others.at[2, span, share],
+                    relay_send.at[k],
+                    relay_recv.at[k],
+                    device,
+                )
+            )
+            relay[k].start()
+
+    last.wait()
+    for copy in second:
+        copy.wait_recv()
+    ready()
     passed = []
-    for d in range(1, grid_x):
-        pieces[d - 1].wait_recv()
-        came = lines.at[(g + grid_x - d) % grid_x, pl.ds(start, part)]
-        passed.append(remote(came, came, pass_send.at[d - 1], pass_recv.at[d - 1], mate))
-        passed[-1].start()
-
+    group = -(-(grid_x - 1) // chunks)
+    for c in range(chunks):
+        for d in range(1 + c * group, min(1 + c * group + group, grid_x)):
+            pieces[d - 1].wait_recv()
+            came = lines.at[(g + grid_x - d) % grid_x, pl.ds(start, part)]
+            passed.append(remote(came, came, pass_send.at[d - 1], pass_recv.at[d - 1], mate))
+            passed[-1].start()
+        relay[2 * c].wait_recv()
+        relay[2 * c + 1].wait_recv()
+        use(c)
     level.wait()
-    last.wait()
-    for copy in second + passed + relay:
-        copy.wait()
-    for copy in own[2:]:
-        copy.wait()
-    for copy in own[:2] + stations + pieces:
-        copy.wait_send()
+    return passed, own + relay + stations + second + pieces + passed
 
 
 def unpack(slot_cap, got, panels, weights, cells):
@@ -240,24 +248,34 @@
     def fill():
         place_kernel(slot_cap, grid_y, owner_row, panels_in, values, spots, sent_slots)
 
-    spread(
-        members, grid_x, grid_y, fill, background, line, sent_slots, others, lines, got, mid,
-        own_send, own_recv, relay_send, relay_recv, line_send, line_recv, hand_send, hand_recv,
-        y_send, y_recv, x_send, x_recv, there,
-    )
-    for copy in fetched:
-        copy.wait()
-    prior[...] = (
-        mixing[m, m] * mine_field[...]
-        + mixing[m, (m + members - 1) % members] * others[0]
-        + mixing[m, (m + 1) % members] * others[1]
-        + mixing[m, (m + 2) % members] * others[2]
-    )
-    unpack(slot_cap, got, panels, weights, cells)
-
     size = 4
     chunks = depth // size
     spans = [pl.ds(c * size, size) for c in range(chunks)]
+
+    seen = []
+
+    def ready():
+        for copy in fetched:
+            copy.wait()
+        unpack(slot_cap, got, panels, weights, cells)
+        seen.extend(masks(cells[...], width_x, width_y))
+
+    def use_prior(c):
+        z = c * size
+        prior[z : z + size] = (
+            mixing[m, m] * mine_field[z : z + size]
+            + mixing[m, (m + members - 1) % members] * others[0, z : z + size]
+            + mixing[m, (m + 1) % members] * others[1, z : z + size]
+            + mixing[m, (m + 2) % members] * others[2, z : z + size]
+        )
+        weights[...] = weights[...] - project(prior, panels, *seen, z)
+
+    passed, unsent = spread(
+        members, grid_x, grid_y, fill, ready, use_prior, background, line, sent_slots, others, lines, got, mid,
+        own_send, own_recv, relay_send, relay_recv, line_send, line_recv, hand_send, hand_recv,
+        y_send, y_recv, x_send, x_recv, there,
+    )
+    at_x, at_y = seen
 
     def start_chunk(source, target, c, k):
         to_far = remote(source, target.at[place, spans[c]], far_send.at[k], far_recv.at[k], far)
@@ -266,87 +284,96 @@
         to_near.start()
         return to_far, to_near
 
-    def solve(target, sent, base, use):
-        passed = []
+    def solve(target, sent, base, use, done):
+        handed = []
 
         def finish(c):
             sent[c][1].wait_recv()
-            passed[c].wait_recv()
+            handed[c].wait_recv()
             for z in range(c * size, c * size + size):
                 rows = jnp.concatenate([target[p, z] for p in range(4)], axis=0)
                 left = jnp.concatenate(halves(lines[z]), axis=0)
                 both = jnp.concatenate(halves(rows), axis=1)
                 full = jnp.dot(left, both, preferred_element_type=F32)
                 use(z, full[:width_x, :width_y] + (full[width_x:, :width_y] + full[:width_x, width_y:]))
+            done(c)
 
         for c in range(chunks):
             sent[c][0].wait_recv()
             came = target.at[other, spans[c]]
-            passed.append(remote(came, came, pass_send.at[base + c], pass_recv.at[base + c], near))
-            passed[c].start()
+            handed.append(remote(came, came, pass_send.at[base + c], pass_recv.at[base + c], near))
+            handed[c].start()
             if c > 0:
                 finish(c - 1)
         finish(chunks - 1)
         for c in range(chunks):
             sent[c][0].wait_send()
             sent[c][1].wait_send()
-            passed[c].wait_send()
-
-    at_x, at_y = masks(cells[...], width_x, width_y)
+            handed[c].wait_send()
+
     lane = lax.broadcasted_iota(jnp.int32, (width_x, width_y), 1)
     row = lax.broadcasted_iota(jnp.int32, (width_x, width_y), 0)
-    weights[...] = weights[...] - project(prior, panels, at_x, at_y)
     sent = []
     for c in range(chunks):
         whole[place, spans[c]] = scattered(weights[...], panels, at_x, at_y, c * size)
         sent.append(start_chunk(whole.at[place, spans[c]], whole, c, c))
 
+    for copy in passed:
+        copy.wait_recv()
     rims = [jnp.zeros((width_x, width_y), F32)]
+    edges = []
 
     def use_first(z, level):
+        c, j = z // size, z % size
         first[z] = level
         scaled = scaling[z] * level
-        x_rim[z : z + 1] = scaled[:1]
-        x_rim[depth + z : depth + z + 1] = scaled[width_x - 1 :]
-        low = jnp.where(lane == z, scaled[:, :1], rims[0])
-        rims[0] = jnp.where(lane == depth + z, scaled[:, width_y - 1 :], low)
-
-    solve(whole, sent, 0, use_first)
-    y_rim[...] = rims[0]
-    edges = [
-        remote(source, target, rim_send.at[k], rim_recv.at[k], device)
-        for k, (source, target, device) in enumerate(
+        x_rim[c, j : j + 1] = scaled[:1]
+        x_rim[c, size + j : size + j + 1] = scaled[width_x - 1 :]
+        low = jnp.where(lane == j, scaled[:, :1], rims[0])
+        rims[0] = jnp.where(lane == size + j, scaled[:, width_y - 1 :], low)
+
+    def send_rims(c):
+        y_rim[c] = rims[0]
+        edges.append(
             [
-                (x_rim, x_low, {"gx": (g + 1) % grid_x}),
-                (x_rim, x_high, {"gx": (g + grid_x - 1) % grid_x}),
-                (y_rim, y_low, up_y),
-                (y_rim, y_high, down_y),
+                remote(source.at[c], target.at[c], rim_send.at[4 * c + k], rim_recv.at[4 * c + k], device)
+                for k, (source, target, device) in enumerate(
+                    [
+                        (x_rim, x_low, {"gx": (g + 1) % grid_x}),
+                        (x_rim, x_high, {"gx": (g + grid_x - 1) % grid_x}),
+                        (y_rim, y_low, up_y),
+                        (y_rim, y_high, down_y),
+                    ]
+                )
             ]
         )
-    ]
-    for copy in edges:
-        copy.start()
-    left = weights[...] - project(first, panels, at_x, at_y)
-    for copy in edges:
-        copy.wait()
-    low_x = jnp.where(g > 0, x_low[...], 0.0)
-    high_x = jnp.where(g < grid_x - 1, x_high[...], 0.0)
-    low_y = jnp.where(h > 0, y_low[...], 0.0)
-    high_y = jnp.where(h < grid_y - 1, y_high[...], 0.0)
+        for copy in edges[c]:
+            copy.start()
+        weights[...] = weights[...] - project(first, panels, at_x, at_y, c * size)
+
+    solve(whole, sent, 0, use_first, send_rims)
+    left = weights[...]
     sent = []
     for c in range(chunks):
         summed = scattered(left, panels, at_x, at_y, c * size)
+        for copy in edges[c]:
+            copy.wait()
+        low_x = jnp.where(g > 0, x_low[c], 0.0)
+        high_x = jnp.where(g < grid_x - 1, x_high[c], 0.0)
+        low_y = jnp.where(h > 0, y_low[c], 0.0)
+        high_y = jnp.where(h < grid_y - 1, y_high[c], 0.0)
         for k in range(c * size, c * size + size):
+            j = k - c * size
             here_u = scaling[k] * first[k]
-            beside = jnp.where(row == 0, low_x[depth + k : depth + k + 1], pltpu.roll(here_u, 1, 0))
+            beside = jnp.where(row == 0, low_x[size + j : size + j + 1], pltpu.roll(here_u, 1, 0))
             beside = beside + jnp.where(
-                row == width_x - 1, high_x[k : k + 1], pltpu.roll(here_u, width_x - 1, 0)
+                row == width_x - 1, high_x[j : j + 1], pltpu.roll(here_u, width_x - 1, 0)
             )
             beside = beside + jnp.where(
-                lane == 0, low_y[:, depth + k : depth + k + 1], pltpu.roll(here_u, 1, 1)
+                lane == 0, low_y[:, size + j : size + j + 1], pltpu.roll(here_u, 1, 1)
             )
             beside = beside + jnp.where(
-                lane == width_y - 1, high_y[:, k : k + 1], pltpu.roll(here_u, width_y - 1, 1)
+                lane == width_y - 1, high_y[:, j : j + 1], pltpu.roll(here_u, width_y - 1, 1)
             )
             if k > 0:
                 beside = beside + scaling[k - 1] * first[k - 1]
@@ -360,7 +387,9 @@
     def use_second(z, level):
         out[z] = first[z] + level
 
-    solve(again, sent, chunks, use_second)
+    solve(again, sent, chunks, use_second, lambda c: None)
+    for copy in unsent:
+        copy.wait_send()
 
 
 def shape(*dims, dtype=F32):
@@ -385,8 +414,8 @@
     packet = pltpu.VMEM((tiles, 2, slot_cap * depth), F32)
     block = pltpu.VMEM((depth, width_x, width_y), F32)
     gathered = pltpu.VMEM((4, depth, width_x, width_y), F32)
-    x_edge = pltpu.VMEM((2 * depth, width_y), F32)
-    y_edge = pltpu.VMEM((width_x, width_y), F32)
+    x_edge = pltpu.VMEM((4, depth // 2, width_y), F32)
+    y_edge = pltpu.VMEM((4, width_x, width_y), F32)
     far_x, far_y = grid_x - 1, grid_y - 1
     prior, second = pl.pallas_call(
         functools.partial(steps_kernel, members, grid_x, grid_y, slot_cap),
@@ -404,9 +433,9 @@
             pltpu.VMEM((1, slots), jnp.int32),
             gathered, gathered, block, pltpu.VMEM((depth, width_x, line), F32), block, block,
             x_edge, y_edge, x_edge, x_edge, y_edge, y_edge,
-            dma(4), dma(4), dma(2), dma(2), dma(far_x), dma(far_x), dma(far_x), dma(far_x),
+            dma(8), dma(8), dma(8), dma(8), dma(far_x), dma(far_x), dma(far_x), dma(far_x),
             dma(far_y), dma(far_y), dma(far_x), dma(far_x), dma(3),
-            dma(8), dma(8), dma(8), dma(8), dma(8), dma(8), dma(4), dma(4), dma(3),
+            dma(8), dma(8), dma(8), dma(8), dma(8), dma(8), dma(16), dma(16), dma(3),
         ],
         compiler_params=pltpu.CompilerParams(collective_id=0, has_side_effects=True),
     )(

time: 77.8 us -> 70.2 us (0.902)
  Pallas kernels: 75.6 us -> 67.9 us
    pallas_call x1, Pallas kernels: 75.6 us -> 67.9 us  [shards(): pl.pallas_call(functools.partial(steps_kernel, members, grid_x, grid_y, s...]
where the time goes in v5:
time: 70.2 us; the launch traced here: 70 us
  Pallas kernels  67.9 us (97%)
  other arithmetic  2.06 us (3%)
    pallas_call x1, Pallas kernels, shards(): pl.pallas_call(functools.partial(steps_kernel, members, grid_x, grid_y, s...  67.9 us
    broadcast_in_dim x1, other arithmetic, shards(): return (prior + second)[None]  2.06 us

profile of v5, /device:TPU:1, one launch (start us, length us, event | category | flops | bytes accessed | tf_op | source)
XLA Modules:
  0.0 70.0 jit_solution(3227327711250914767)
XLA Ops:
  0.0 67.9 %shard_map.91 = (f32[16,64,128]{2,1,0:T(8,128)}, f32[16,64,128]{2,1,0:T(8,128)}) custom-call(f32[4,4]{1,0:T(4,128)} %mixing.1, s32[1,512]{1,0:T(1,128)} %bitcast.8, f32[16,512]{1,0:T(8,128)} %panels_in.1, f32[1,512]{1,0:T(1,128)} %values.1, s32[1,512]{1,0:T(1,128)} %bitcast.9, f32[16,64,128]{2,1,0:T(8,128)} %bitcast.7, f32[4,256,256]{2,1,0:T(8,128)} %bitcast.6, ...), custom_call_target="tpu_custom_call" | custom-call | tf_op jit(solution)/shard_map/pallas_call | solution.py:420
  67.9 2.1 %add_bitcast_fusion = f32[1,16,64,128]{3,2,1,0:T(8,128)} fusion(f32[16,64,128]{2,1,0:T(8,128)} %get-tuple-element.7, f32[16,64,128]{2,1,0:T(8,128)} %get-tuple-element.8), kind=kLoop, calls=%fused_computation | loop fusion | flops 131072 | bytes 1572864 | tf_op jit(solution)/shard_map/broadcast_in_dim | solution.py:445

commit v6 on v5

--- a/solution.py
+++ b/solution.py
@@ -145,7 +145,10 @@
                 along_x[d - 1],
             )
         )
-        pieces[-1].start()
+    order = sorted(range(grid_x - 1), key=lambda k: min(k + 1, grid_x - 1 - k))
+    early, late = order[: grid_x // 2], order[grid_x // 2 :]
+    for k in early:
+        pieces[k].start()
     mine_rows = pl.ds(pl.multiple_of((g % quads) * wide, wide), wide)
     level = pltpu.make_async_copy(line.at[g // quads, mine_rows], lines.at[g], here.at[1])
     level.start()
@@ -170,6 +173,8 @@
         copy.start()
     last = pltpu.make_async_copy(mid.at[:, g], got.at[pl.ds(g * grid_y, grid_y)], here.at[2])
     last.start()
+    for k in late:
+        pieces[k].start()
 
     relay = []
     rows = background.shape[1] // 2
@@ -194,16 +199,21 @@
         copy.wait_recv()
     ready()
     passed = []
-    group = -(-(grid_x - 1) // chunks)
+
+    def hand_over(k):
+        pieces[k].wait_recv()
+        came = lines.at[(g + grid_x - 1 - k) % grid_x, pl.ds(start, part)]
+        passed.append(remote(came, came, pass_send.at[k], pass_recv.at[k], mate))
+        passed[-1].start()
+
+    for k in early:
+        hand_over(k)
     for c in range(chunks):
-        for d in range(1 + c * group, min(1 + c * group + group, grid_x)):
-            pieces[d - 1].wait_recv()
-            came = lines.at[(g + grid_x - d) % grid_x, pl.ds(start, part)]
-            passed.append(remote(came, came, pass_send.at[d - 1], pass_recv.at[d - 1], mate))
-            passed[-1].start()
         relay[2 * c].wait_recv()
         relay[2 * c + 1].wait_recv()
         use(c)
+    for k in late:
+        hand_over(k)
     level.wait()
     return passed, own + relay + stations + second + pieces + passed
 

time: 70.2 us -> 70.9 us (level); the launches traced: 70 us -> 69.8 us
  no operation moved by 1% of the time
where the time goes in v6:
time: 70.9 us; the launch traced here: 69.8 us
  Pallas kernels  67.7 us (95%)
  other arithmetic  2.06 us (3%)
    pallas_call x1, Pallas kernels, shards(): pl.pallas_call(functools.partial(steps_kernel, members, grid_x, grid_y, s...  67.7 us
    broadcast_in_dim x1, other arithmetic, shards(): return (prior + second)[None]  2.06 us

profile of v6, /device:TPU:1, one launch (start us, length us, event | category | flops | bytes accessed | tf_op | source)
XLA Modules:
  0.0 69.8 jit_solution(4781160241023098334)
XLA Ops:
  0.0 67.7 %shard_map.91 = (f32[16,64,128]{2,1,0:T(8,128)}, f32[16,64,128]{2,1,0:T(8,128)}) custom-call(f32[4,4]{1,0:T(4,128)} %mixing.1, s32[1,512]{1,0:T(1,128)} %bitcast.8, f32[16,512]{1,0:T(8,128)} %panels_in.1, f32[1,512]{1,0:T(1,128)} %values.1, s32[1,512]{1,0:T(1,128)} %bitcast.9, f32[16,64,128]{2,1,0:T(8,128)} %bitcast.7, f32[4,256,256]{2,1,0:T(8,128)} %bitcast.6, ...), custom_call_target="tpu_custom_call" | custom-call | tf_op jit(solution)/shard_map/pallas_call | solution.py:430
  67.7 2.1 %add_bitcast_fusion = f32[1,16,64,128]{3,2,1,0:T(8,128)} fusion(f32[16,64,128]{2,1,0:T(8,128)} %get-tuple-element.7, f32[16,64,128]{2,1,0:T(8,128)} %get-tuple-element.8), kind=kLoop, calls=%fused_computation | loop fusion | flops 131072 | bytes 1572864 | tf_op jit(solution)/shard_map/broadcast_in_dim | solution.py:455
